TPU v7x, 32 devices: a whole 2x2x4 slice. The times are simulated.
32 devices in a mesh: fsdp: 2 (over y), ctx: 4 (over z), tp: 4 (over x, core).
Axes of the slice: x: 2, y: 2, z: 4, core: 2. Of those that a mesh axis runs over, the one named last changes fastest.
Arguments:
- tokens: bfloat16 [5120, 2, 1024], P(('ctx', 'tp'), 'fsdp'), may hold values from -6 to 6
- first_values: bfloat16 [5120, 2, 1024], P('ctx', 'fsdp', 'tp'), may hold values from -6 to 6
- cotangent: bfloat16 [5120, 2, 1024], P(('ctx', 'tp'), 'fsdp'), may hold values from -6 to 6
- parents: int32 [2, 13], P('fsdp'), may hold values from 0 to 11, as said below
- seg_lengths: int32 [2, 13], P('fsdp'), may hold values from 1 to 2048, 5120 in all within a row
- w_query: bfloat16 [1024, 1024], P('fsdp', 'tp'), may hold values from -0.1875 to 0.1875
- w_key: bfloat16 [1024, 1024], P('fsdp', 'tp'), may hold values from -0.1875 to 0.1875
- w_value: bfloat16 [1024, 1024], P('fsdp', 'tp'), may hold values from -0.1875 to 0.1875
- w_out: bfloat16 [1024, 1024], P('fsdp', 'tp'), may hold values from -1.5 to 1.5
- w_gate: bfloat16 [1024, 2816], P('fsdp', 'tp'), may hold values from -0.1875 to 0.1875
- w_up: bfloat16 [1024, 2816], P('fsdp', 'tp'), may hold values from -0.1875 to 0.1875
- w_down: bfloat16 [1024, 2816], P('fsdp', 'tp'), may hold values from -0.109375 to 0.109375
- gain_attn: bfloat16 [1024], P('fsdp'), may hold values from 0.5 to 1.5
- gain_ffn: bfloat16 [1024], P('fsdp'), may hold values from 0.5 to 1.5
Outputs:
- layer_out: bfloat16 [5120, 2, 1024], P(('ctx', 'tp'), 'fsdp')
- grad_tokens: float32 [5120, 2, 1024], P(('ctx', 'tp'), 'fsdp')
- grad_values: float32 [5120, 2, 1024], P('ctx', 'fsdp', 'tp')
- grad_query: float32 [1024, 1024], P('fsdp', 'tp')
- grad_key: float32 [1024, 1024], P('fsdp', 'tp')
- grad_value: float32 [1024, 1024], P('fsdp', 'tp')
- grad_out: float32 [1024, 1024], P('fsdp', 'tp')
- grad_gate: float32 [1024, 2816], P('fsdp', 'tp')
- grad_up: float32 [1024, 2816], P('fsdp', 'tp')
- grad_down: float32 [1024, 2816], P('fsdp', 'tp')
- grad_gain_attn: float32 [1024], P('fsdp')
- grad_gain_ffn: float32 [1024], P('fsdp')
Inputs may be any that keep to these rules, and one draw needn't show every extreme that they name: `parents`: segment 0 of each tree is its root and names itself; every other segment's parent comes before it, at most 4 places back; the last segment's parent is the one just before it.
All inputs are finite; a program needn't handle non-finite values.
Results may differ from a plain program's by a relative error of at most 0.022.
Values may be sent and summed in bfloat16 or wider, within the bound.
No kernel may reach another device: no remote copies, remote signals or barrier semaphores. Data moves between devices by JAX's collectives and lax.ppermute only.
A program may use at most 192 MiB of HBM per device.

v0:
```python
import math

import jax
import jax.numpy as jnp
from jax import lax
from jax.sharding import PartitionSpec as P

HEAD = 64
TREE_LEN = 5120


epsilon = 1e-05
masked_score = -1e30
highest = lax.Precision.HIGHEST


def rms_scale(values, scale_gain):
    return (
        values * lax.rsqrt(jnp.mean(values * values, axis=-1, keepdims=True) + epsilon) * scale_gain
    )


def gated(joined):
    middle_at = joined.shape[-1] // 2
    return jax.nn.silu(joined[..., :middle_at]) * joined[..., middle_at:]


def keep_same(running):
    return running


def rotary(values, position, direction):
    half_head = HEAD // 2
    frequency = jnp.exp(-math.log(10000.0) * jnp.arange(half_head, dtype=jnp.float32) / half_head)
    angles = position[..., None] * frequency
    cosine = jnp.cos(angles)[..., None, :]
    sine_term = direction * jnp.sin(angles)[..., None, :]
    shaped = values.reshape(values.shape[:-1] + (values.shape[-1] // HEAD, HEAD))
    first_half = shaped[..., :half_head]
    second_half = shaped[..., half_head:]
    rotated = jnp.concatenate(
        [
            first_half * cosine - second_half * sine_term,
            second_half * cosine + first_half * sine_term,
        ],
        axis=-1,
    )
    return rotated.reshape(values.shape)


def tree_layout(parents, lengths):
    seg_count = parents.shape[-1]
    seg_index = jnp.arange(seg_count, dtype=jnp.int32)
    parent_link = (
        (parents[:, :, None] == seg_index[None, None, :]) & (seg_index[None, :, None] > 0)
    ).astype(jnp.float32)
    identity = jnp.eye(seg_count, dtype=jnp.float32)

    def climb_step(step_at, ancestors):
        return jnp.minimum(
            identity + jnp.einsum("bst,btu->bsu", parent_link, ancestors, precision=highest), 1.0
        )

    ancestors = lax.fori_loop(
        0, seg_count, climb_step, jnp.broadcast_to(identity, parent_link.shape)
    )
    offsets = jnp.cumsum(lengths, axis=-1) - lengths
    above_len = jnp.einsum(
        "bsu,bu->bs", ancestors - identity, lengths.astype(jnp.float32), precision=highest
    )
    token_index = jnp.arange(TREE_LEN, dtype=jnp.int32)
    token_segment = (
        jnp.sum((offsets[:, None, :] <= token_index[None, :, None]).astype(jnp.int32), axis=-1) - 1
    )
    membership = (token_segment[:, :, None] == seg_index[None, None, :]).astype(jnp.float32)
    seg_start = jnp.einsum("bts,bs->bt", membership, offsets.astype(jnp.float32), precision=highest)
    seg_depth = jnp.einsum("bts,bs->bt", membership, above_len, precision=highest)
    position = token_index.astype(jnp.float32)[None, :] - seg_start + seg_depth
    return (membership, ancestors, position)


def on_device(
    tokens,
    first_values,
    cotangent,
    parents,
    seg_lengths,
    w_query,
    w_key,
    w_value,
    w_out,
    w_gate,
    w_up,
    w_down,
    gain_attn,
    gain_ffn,
):
    local_rows = tokens.shape[0]
    ctx_count = lax.axis_size("ctx")
    ctx_place = lax.axis_index("ctx")
    block_rows = local_rows * lax.axis_size("tp")
    head_width = w_query.shape[1]
    local_heads = head_width // HEAD
    score_scale = HEAD ** (-0.5)
    membership, ancestors, position = tree_layout(parents, seg_lengths)
    ancestry = jnp.einsum("bts,bsu->btu", membership, ancestors, precision=highest)
    row_begin = ctx_place * block_rows
    own_position = jnp.transpose(lax.dynamic_slice_in_dim(position, row_begin, block_rows, 1))
    own_ancestry = lax.dynamic_slice_in_dim(ancestry, row_begin, block_rows, 1)
    query_index = row_begin + jnp.arange(block_rows, dtype=jnp.int32)

    def fetch_weights():
        fetched = list(
            (
                lax.all_gather(w_query, "fsdp", axis=0, tiled=True),
                lax.all_gather(w_key, "fsdp", axis=0, tiled=True),
                lax.all_gather(w_value, "fsdp", axis=0, tiled=True),
                lax.all_gather(w_out, "fsdp", axis=0, tiled=True),
                lax.all_gather(w_gate, "fsdp", axis=0, tiled=True),
                lax.all_gather(w_up, "fsdp", axis=0, tiled=True),
                lax.all_gather(w_down, "fsdp", axis=0, tiled=True),
                lax.all_gather(gain_attn, "fsdp", axis=0, tiled=True),
                lax.all_gather(gain_ffn, "fsdp", axis=0, tiled=True),
            )
        )
        qkv_weight = jnp.concatenate(fetched[:3], axis=1)
        joint_weight = jnp.concatenate(fetched[4:6], axis=1)
        return (
            qkv_weight,
            fetched[3],
            joint_weight,
            fetched[6],
            fetched[7].astype(jnp.float32),
            fetched[8].astype(jnp.float32),
        )

    def gather_rows(values):
        return lax.all_gather(values, "tp", axis=0, tiled=True)

    def sum_rows(operand, weight):
        return lax.psum_scatter(
            jnp.einsum("rbk,dk->rbd", operand, weight, preferred_element_type=jnp.float32).astype(
                jnp.bfloat16
            ),
            "tp",
            scatter_dimension=0,
            tiled=True,
        ).astype(jnp.float32)

    def by_heads(array):
        return array.reshape(array.shape[0], local_heads, HEAD)

    def key_piece(row_source, tree_at, piece_at):
        return by_heads(row_source[piece_at * block_rows : (piece_at + 1) * block_rows, tree_at])

    def piece_mask(tree_at, piece_at):
        piece_members = membership[tree_at, piece_at * block_rows : (piece_at + 1) * block_rows]
        linked = (
            jnp.dot(own_ancestry[tree_at], jnp.transpose(piece_members), precision=highest) > 0.5
        )
        key_index = piece_at * block_rows + jnp.arange(block_rows, dtype=jnp.int32)
        return linked & (key_index[None, :] <= query_index[:, None])

    def over_pieces(tree_at, query_heads, key_source, step, running):
        for piece_at in range(ctx_count):

            def visit_piece(partial_state, piece_at=piece_at):
                allowed = piece_mask(tree_at, piece_at)
                raw_scores = (
                    jnp.einsum(
                        "qhd,khd->hqk",
                        query_heads,
                        key_piece(key_source, tree_at, piece_at),
                        preferred_element_type=jnp.float32,
                    )
                    * score_scale
                )
                scores = jnp.where(allowed[None], raw_scores, masked_score)
                return step(partial_state, piece_at, allowed, scores)

            running = lax.cond(piece_at <= ctx_place, visit_piece, keep_same, running)
        return running

    qkv_weight, out_weight, joint_weight, down_weight, attention_gain, ffn_gain = fetch_weights()
    single_tokens = tokens.astype(jnp.float32)
    normed_own = rms_scale(single_tokens, attention_gain).astype(jnp.bfloat16)
    normed_rows = gather_rows(normed_own)
    projected = jnp.einsum(
        "rbd,dk->rbk", normed_rows, qkv_weight, preferred_element_type=jnp.float32
    )
    queries = rotary(projected[..., :head_width], own_position, 1.0).astype(jnp.bfloat16)
    key_vectors = rotary(projected[..., head_width : 2 * head_width], own_position, 1.0).astype(
        jnp.bfloat16
    )
    values = (
        0.5 * projected[..., 2 * head_width :] + 0.5 * first_values.astype(jnp.float32)
    ).astype(jnp.bfloat16)

    def fetch_keys():
        return (
            lax.all_gather(key_vectors, "ctx", axis=0, tiled=True),
            lax.all_gather(values, "ctx", axis=0, tiled=True),
        )

    key_rows, value_rows = fetch_keys()
    tree_at = 0
    query_heads = by_heads(queries[:, tree_at])

    def stats_step(partial_state, piece_at, allowed, scores):
        running_top, running_total = partial_state
        new_top = jnp.maximum(running_top, jnp.max(scores, axis=-1))
        weight_terms = jnp.where(allowed[None], jnp.exp(scores - new_top[..., None]), 0.0)
        return (
            new_top,
            running_total * jnp.exp(running_top - new_top) + jnp.sum(weight_terms, axis=-1),
        )

    start_state = (
        jnp.full((local_heads, block_rows), masked_score, jnp.float32),
        jnp.zeros((local_heads, block_rows), jnp.float32),
    )
    top_final, total_final = over_pieces(tree_at, query_heads, key_rows, stats_step, start_state)
    log_total = top_final + jnp.log(total_final)

    def mix_step(accumulated, piece_at, allowed, scores, log_total=log_total, tree_at=tree_at):
        probability = jnp.where(allowed[None], jnp.exp(scores - log_total[..., None]), 0.0).astype(
            jnp.bfloat16
        )
        return accumulated + jnp.einsum(
            "hqk,khd->qhd",
            probability,
            key_piece(value_rows, tree_at, piece_at),
            preferred_element_type=jnp.float32,
        )

    mixed_tree = over_pieces(
        tree_at,
        query_heads,
        key_rows,
        mix_step,
        jnp.zeros((block_rows, local_heads, HEAD), jnp.float32),
    )
    totals_list = [log_total]
    mixed_list = [mixed_tree.reshape(block_rows, head_width)]
    mixed_single = jnp.stack(mixed_list, axis=1)
    mixed_low = mixed_single.astype(jnp.bfloat16)
    middle_state = single_tokens + sum_rows(mixed_low, out_weight)
    ffn_normed = rms_scale(middle_state, ffn_gain).astype(jnp.bfloat16)
    ffn_input = gather_rows(ffn_normed)
    joined = jnp.einsum("rbd,dk->rbk", ffn_input, joint_weight, preferred_element_type=jnp.float32)
    hidden = gated(joined).astype(jnp.bfloat16)
    ffn_result = sum_rows(hidden, down_weight)
    layer_out = (middle_state + ffn_result).astype(jnp.bfloat16)
    qkv_weight, out_weight, joint_weight, down_weight, attention_gain, ffn_gain = fetch_weights()
    cot_input = gather_rows(cotangent)
    hidden_grad = jnp.einsum(
        "rbd,dk->rbk", cot_input, down_weight, preferred_element_type=jnp.float32
    )
    joined_grad = jax.vjp(gated, joined)[1](hidden_grad)[0].astype(jnp.bfloat16)
    grad_joint = jnp.einsum(
        "rbd,rbk->dk", ffn_input, joined_grad, preferred_element_type=jnp.float32
    )
    grad_down = jnp.einsum("rbd,rbk->dk", cot_input, hidden, preferred_element_type=jnp.float32)
    ffn_normed_grad = sum_rows(joined_grad, joint_weight)
    gate_width = grad_joint.shape[1] // 2
    grad_gate = grad_joint[:, :gate_width]
    grad_up = grad_joint[:, gate_width:]
    middle_grad, ffn_gain_grad = jax.vjp(rms_scale, middle_state, ffn_gain)[1](ffn_normed_grad)
    middle_grad = middle_grad + cotangent.astype(jnp.float32)
    middle_rows = gather_rows(middle_grad.astype(jnp.bfloat16))
    out_grad = jnp.einsum(
        "rbd,dk->rbk", middle_rows, out_weight, preferred_element_type=jnp.float32
    ).astype(jnp.bfloat16)
    grad_out = jnp.einsum("rbd,rbk->dk", middle_rows, mixed_low, preferred_element_type=jnp.float32)
    key_back, value_back = fetch_keys()
    tree_at = 0
    query_heads = by_heads(queries[:, tree_at])
    grad_heads = by_heads(out_grad[:, tree_at])
    log_total = totals_list[tree_at]
    delta_term = jnp.einsum(
        "qhd,qhd->hq", grad_heads.astype(jnp.float32), by_heads(mixed_single[:, tree_at])
    )

    def back_step(
        partial_state,
        piece_at,
        allowed,
        scores,
        tree_at=tree_at,
        query_heads=query_heads,
        grad_heads=grad_heads,
        log_total=log_total,
        delta_term=delta_term,
    ):
        query_grad, key_parts, value_parts = partial_state
        probability = jnp.where(allowed[None], jnp.exp(scores - log_total[..., None]), 0.0)
        value_piece = key_piece(value_back, tree_at, piece_at)
        key_heads = key_piece(key_back, tree_at, piece_at)
        value_grad = jnp.einsum(
            "hqk,qhd->khd",
            probability.astype(jnp.bfloat16),
            grad_heads,
            preferred_element_type=jnp.float32,
        )
        prob_grad = jnp.einsum(
            "qhd,khd->hqk", grad_heads, value_piece, preferred_element_type=jnp.float32
        )
        score_grad = (probability * (prob_grad - delta_term[..., None])).astype(jnp.bfloat16)
        query_grad = (
            query_grad
            + jnp.einsum("hqk,khd->qhd", score_grad, key_heads, preferred_element_type=jnp.float32)
            * score_scale
        )
        key_grad = (
            jnp.einsum("hqk,qhd->khd", score_grad, query_heads, preferred_element_type=jnp.float32)
            * score_scale
        )
        key_parts = key_parts[:piece_at] + (key_grad,) + key_parts[piece_at + 1 :]
        value_parts = value_parts[:piece_at] + (value_grad,) + value_parts[piece_at + 1 :]
        return (query_grad, key_parts, value_parts)

    zero_piece = jnp.zeros((block_rows, local_heads, HEAD), jnp.float32)
    start_state = (
        zero_piece,
        tuple((zero_piece for piece_at in range(ctx_count))),
        tuple((zero_piece for piece_at in range(ctx_count))),
    )
    query_grad, key_parts, value_parts = over_pieces(
        tree_at, query_heads, key_back, back_step, start_state
    )
    query_grads = [query_grad.reshape(block_rows, head_width)]
    key_grad_trees = [jnp.concatenate(key_parts, axis=0).reshape(-1, head_width)]
    value_grad_trees = [jnp.concatenate(value_parts, axis=0).reshape(-1, head_width)]
    key_grad_own, value_grad_own = (
        lax.psum_scatter(
            jnp.stack(key_grad_trees, axis=1).astype(jnp.bfloat16),
            "ctx",
            scatter_dimension=0,
            tiled=True,
        ).astype(jnp.float32),
        lax.psum_scatter(
            jnp.stack(value_grad_trees, axis=1).astype(jnp.bfloat16),
            "ctx",
            scatter_dimension=0,
            tiled=True,
        ).astype(jnp.float32),
    )
    grad_values = 0.5 * value_grad_own
    query_grad_all = jnp.stack(query_grads, axis=1)
    projected_grad = jnp.concatenate(
        [
            rotary(query_grad_all, own_position, -1.0),
            rotary(key_grad_own, own_position, -1.0),
            grad_values,
        ],
        axis=-1,
    ).astype(jnp.bfloat16)
    grad_qkv = jnp.einsum(
        "rbd,rbk->dk", normed_rows, projected_grad, preferred_element_type=jnp.float32
    )
    normed_grad = sum_rows(projected_grad, qkv_weight)
    token_grad, attention_gain_grad = jax.vjp(rms_scale, single_tokens, attention_gain)[1](
        normed_grad
    )
    token_grad = token_grad + middle_grad
    owned = (
        lax.psum_scatter(
            grad_qkv[:, :head_width].astype(jnp.bfloat16), "fsdp", scatter_dimension=0, tiled=True
        ).astype(jnp.float32),
        lax.psum_scatter(
            grad_qkv[:, head_width : 2 * head_width].astype(jnp.bfloat16),
            "fsdp",
            scatter_dimension=0,
            tiled=True,
        ).astype(jnp.float32),
        lax.psum_scatter(
            grad_qkv[:, 2 * head_width :].astype(jnp.bfloat16),
            "fsdp",
            scatter_dimension=0,
            tiled=True,
        ).astype(jnp.float32),
        lax.psum_scatter(
            grad_out.astype(jnp.bfloat16), "fsdp", scatter_dimension=0, tiled=True
        ).astype(jnp.float32),
        lax.psum_scatter(
            grad_gate.astype(jnp.bfloat16), "fsdp", scatter_dimension=0, tiled=True
        ).astype(jnp.float32),
        lax.psum_scatter(
            grad_up.astype(jnp.bfloat16), "fsdp", scatter_dimension=0, tiled=True
        ).astype(jnp.float32),
        lax.psum_scatter(
            grad_down.astype(jnp.bfloat16), "fsdp", scatter_dimension=0, tiled=True
        ).astype(jnp.float32),
        lax.psum_scatter(
            attention_gain_grad.astype(jnp.bfloat16), "fsdp", scatter_dimension=0, tiled=True
        ).astype(jnp.float32),
        lax.psum_scatter(
            ffn_gain_grad.astype(jnp.bfloat16), "fsdp", scatter_dimension=0, tiled=True
        ).astype(jnp.float32),
    )
    owned = (
        lax.psum(owned[0].astype(jnp.bfloat16), "ctx").astype(jnp.float32),
        lax.psum(owned[1].astype(jnp.bfloat16), "ctx").astype(jnp.float32),
        lax.psum(owned[2].astype(jnp.bfloat16), "ctx").astype(jnp.float32),
        lax.psum(owned[3].astype(jnp.bfloat16), "ctx").astype(jnp.float32),
        lax.psum(owned[4].astype(jnp.bfloat16), "ctx").astype(jnp.float32),
        lax.psum(owned[5].astype(jnp.bfloat16), "ctx").astype(jnp.float32),
        lax.psum(owned[6].astype(jnp.bfloat16), "ctx").astype(jnp.float32),
        lax.psum(owned[7].astype(jnp.bfloat16), "ctx").astype(jnp.float32),
        lax.psum(owned[8].astype(jnp.bfloat16), "ctx").astype(jnp.float32),
    )
    gain_grads = lax.psum((owned[7], owned[8]), "tp")
    return (
        layer_out,
        token_grad,
        grad_values,
        owned[0],
        owned[1],
        owned[2],
        owned[3],
        owned[4],
        owned[5],
        owned[6],
        gain_grads[0],
        gain_grads[1],
    )


def solution(mesh):
    placed = (
        P(("ctx", "tp"), "fsdp", None),
        P("ctx", "fsdp", "tp"),
        P(("ctx", "tp"), "fsdp", None),
        P("fsdp", None),
        P("fsdp", None),
        P("fsdp", "tp"),
        P("fsdp", "tp"),
        P("fsdp", "tp"),
        P("fsdp", "tp"),
        P("fsdp", "tp"),
        P("fsdp", "tp"),
        P("fsdp", "tp"),
        P("fsdp"),
        P("fsdp"),
    )
    return jax.shard_map(
        on_device,
        mesh=mesh,
        in_specs=placed,
        out_specs=(
            P(("ctx", "tp"), "fsdp", None),
            P(("ctx", "tp"), "fsdp", None),
            P("ctx", "fsdp", "tp"),
            P("fsdp", "tp"),
            P("fsdp", "tp"),
            P("fsdp", "tp"),
            P("fsdp", "tp"),
            P("fsdp", "tp"),
            P("fsdp", "tp"),
            P("fsdp", "tp"),
            P("fsdp"),
            P("fsdp"),
        ),
        check_vma=False,
    )
```

profile of v0, /device:TPU:0, one launch (start us, length us, event | category | flops | bytes accessed | tf_op | source)
XLA Modules:
  0.0 1294.7 jit_solution(10947846499127552712)
XLA Ops:
  64.1 47.5 %all-gather.14.cloned.1.call-done = bf16[5120,1,256]{0,2,1:T(8,128)(2,1)} async-done(((bf16[1280,1,256]{0,2,1:T(8,128)(2,1)}), bf16[5120,1,256]{0,2,1:T(8,128)(2,1)}) %all-gather.14.cloned.1.call-update) | async-done | bytes 2621456 | tf_op jit(solution)/shard_map/all_gather | solution.py:201
  111.6 38.5 %conditional.12 = (f32[4,1280]{1,0:T(4,128)}, f32[4,1280]{1,0:T(4,128)S(1)}) conditional(s32[]{:T(128)} %convert_element_type.323, () %tuple.108, (f32[1,1280,13]{1,0,2:T(1,128)S(1)}, f32[1,5120,13]{1,0,2:T(1,128)S(1)}, s32[1280]{0:T(1024)S(1)}, bf16[5120,1,256]{0,2,1:T(8,128)(2,1)}, bf16[1280,4,64]{0,2,1:T(8,128)(2,1)S(1)}) %tuple.109), branch_computations={%region_5.6_spmd, %region_6.9_spmd} | conditional | flops 1138703360 | bytes 63677456 | solution.py:181
  125.5 12.4 fusion.253
  168.4 22.8 %conditional.16 = (f32[1280,4,64]{0,2,1:T(8,128)S(1)}) conditional(s32[]{:T(128)} %convert_element_type.323, () %tuple.106, (f32[1,1280,13]{1,0,2:T(1,128)S(1)}, f32[1,5120,13]{1,0,2:T(1,128)S(1)}, s32[1280]{0:T(1024)S(1)}, bf16[5120,1,256]{0,2,1:T(8,128)(2,1)}, bf16[1280,4,64]{0,2,1:T(8,128)(2,1)S(1)}, /*index=5*/f32[4,1280]{1,0:T(4,128)S(1)}, ...), branch_computations={%region_21.22_spmd, %region_22.23_spmd} | conditional | flops 1970995200 | bytes 9466888 | solution.py:181
  178.9 12.2 convolution_bitcast_fusion
  214.6 185.4 %reduce-scatter.14.cloned.1.call-done = bf16[320,1,1024]{2,0,1:T(8,128)(2,1)} async-done(((bf16[1280,1,1024]{2,0,1:T(8,128)(2,1)}), bf16[320,1,1024]{2,0,1:T(8,128)(2,1)}) %reduce-scatter.14.cloned.1.call-update) | async-done | bytes 655376 | tf_op jit(solution)/shard_map/reduce_scatter | solution.py:141
  422.4 24.9 %all-gather.18.cloned.1.call-done = bf16[1280,1,1024]{2,0,1:T(8,128)(2,1)} async-done(((bf16[320,1,1024]{2,0,1:T(8,128)(2,1)}), bf16[1280,1,1024]{2,0,1:T(8,128)(2,1)}) %all-gather.18.cloned.1.call-update) | async-done | bytes 2621456 | tf_op jit(solution)/shard_map/all_gather | solution.py:138
  457.1 17.4 %all-gather.24.cloned.1.call-done = bf16[1024,704]{0,1:T(8,128)(2,1)} async-done(((bf16[512,704]{0,1:T(8,128)(2,1)}), bf16[1024,704]{0,1:T(8,128)(2,1)}) %all-gather.24.cloned.1.call-update) | async-done | bytes 1441808 | tf_op jit(solution)/shard_map/all_gather | solution.py:121
  474.5 27.1 %all-gather.26.cloned.1.call-done = bf16[1280,1,1024]{2,0,1:T(8,128)(2,1)} async-done(((bf16[320,1,1024]{2,0,1:T(8,128)(2,1)}), bf16[1280,1,1024]{2,0,1:T(8,128)(2,1)}) %all-gather.26.cloned.1.call-update) | async-done | bytes 2621456 | tf_op jit(solution)/shard_map/all_gather | solution.py:138
  519.7 34.7 %reduce-scatter.18.cloned.1.call-done = bf16[320,1,1024]{2,0,1:T(8,128)(2,1)} async-done(((bf16[1280,1,1024]{2,0,1:T(8,128)(2,1)}), bf16[320,1,1024]{2,0,1:T(8,128)(2,1)}) %reduce-scatter.18.cloned.1.call-update) | async-done | bytes 655376 | tf_op jit(solution)/shard_map/reduce_scatter | solution.py:141
  559.4 25.4 %all-gather.28.cloned.1.call-done = bf16[1280,1,1024]{2,0,1:T(8,128)(2,1)} async-done(((bf16[320,1,1024]{2,0,1:T(8,128)(2,1)}), bf16[1280,1,1024]{2,0,1:T(8,128)(2,1)}) %all-gather.28.cloned.1.call-update) | async-done | bytes 2621456 | tf_op jit(solution)/shard_map/all_gather | solution.py:138
  587.9 65.5 %conditional.20 = (f32[1280,4,64]{0,2,1:T(8,128)S(1)}, bf16[1280,4,64]{0,2,1:T(8,128)(2,1)}, bf16[1280,4,64]{0,2,1:T(8,128)(2,1)}) conditional(s32[]{:T(128)} %convert_element_type.323, () %tuple.117, (f32[1,1280,13]{1,0,2:T(1,128)S(1)}, f32[1,5120,13]{1,0,2:T(1,128)S(1)}, s32[1280]{0:T(1024)S(1)}, bf16[5120,1,256]{0,2,1:T(8,128)(2,1)}, ...), branch_computations={%region_34.35_spmd, %region_35.36_spmd} | conditional | flops 4508549120 | bytes 134005808 | solution.py:181
  597.0 12.6 fusion.81
  621.3 15.2 %fusion.82 = bf16[4,1280,1280]{2,1,0:T(8,128)(2,1)} fusion(f32[4,1280,1280]{2,1,0:T(8,128)} %fusion.81, bf16[1280,4,64]{0,2,1:T(8,128)(2,1)S(1)} %get-tuple-element.316, bf16[1280,4,64]{0,2,1:T(8,128)(2,1)S(1)} %bitcast.342, f32[4,1280]{1,0:T(4,128)S(1)} %get-tuple-element.318), kind=kOutput, calls=%fused_computation.125 | convolution fusion | flops 858521600 | bytes 40652800 | tf_op jit(solution)/shard_map/cond/branch_1_fun/qhd,khd->hqk/dot_general | solution.py:305
  712.7 193.9 %reduce-scatter.20.cloned.1.call-done = bf16[1280,1,256]{0,2,1:T(8,128)(2,1)} async-done(((bf16[5120,1,256]{0,2,1:T(8,128)(2,1)}), bf16[1280,1,256]{0,2,1:T(8,128)(2,1)}) %reduce-scatter.20.cloned.1.call-update) | async-done | bytes 655376 | tf_op jit(solution)/shard_map/reduce_scatter | solution.py:335
  909.1 51.6 %reduce-scatter.22.cloned.1.call-done = bf16[1280,1,256]{0,2,1:T(8,128)(2,1)} async-done(((bf16[5120,1,256]{0,2,1:T(8,128)(2,1)}), bf16[1280,1,256]{0,2,1:T(8,128)(2,1)}) %reduce-scatter.22.cloned.1.call-update) | async-done | bytes 655376 | tf_op jit(solution)/shard_map/reduce_scatter | solution.py:341
  967.6 20.4 %reduce-scatter.38.cloned.1.call-done = bf16[512,704]{0,1:T(8,128)(2,1)} async-done(((bf16[1024,704]{0,1:T(8,128)(2,1)}), bf16[512,704]{0,1:T(8,128)(2,1)}) %reduce-scatter.38.cloned.1.call-update) | async-done | bytes 720912 | tf_op jit(solution)/shard_map/reduce_scatter | solution.py:391
  987.9 28.4 %reduce-scatter.36.cloned.1.call-done = bf16[512,704]{1,0:T(8,128)(2,1)} async-done(((bf16[1024,704]{1,0:T(8,128)(2,1)}), bf16[512,704]{1,0:T(8,128)(2,1)}) %reduce-scatter.36.cloned.1.call-update) | async-done | bytes 720912 | tf_op jit(solution)/shard_map/reduce_scatter | solution.py:388
  1016.4 28.2 %reduce-scatter.34.cloned.1.call-done = bf16[512,704]{1,0:T(8,128)(2,1)} async-done(((bf16[1024,704]{1,0:T(8,128)(2,1)}), bf16[512,704]{1,0:T(8,128)(2,1)}) %reduce-scatter.34.cloned.1.call-update) | async-done | bytes 720912 | tf_op jit(solution)/shard_map/reduce_scatter | solution.py:385
  1044.6 17.5 %reduce-scatter.32.cloned.1.call-done = bf16[512,256]{1,0:T(8,128)(2,1)} async-done(((bf16[1024,256]{1,0:T(8,128)(2,1)}), bf16[512,256]{1,0:T(8,128)(2,1)}) %reduce-scatter.32.cloned.1.call-update) | async-done | bytes 262160 | tf_op jit(solution)/shard_map/reduce_scatter | solution.py:382
  1062.1 17.2 %reduce-scatter.30.cloned.1.call-done = bf16[512,256]{1,0:T(8,128)(2,1)} async-done(((bf16[1024,256]{1,0:T(8,128)(2,1)}), bf16[512,256]{1,0:T(8,128)(2,1)}) %reduce-scatter.30.cloned.1.call-update) | async-done | bytes 262160 | tf_op jit(solution)/shard_map/reduce_scatter | solution.py:376
  1079.3 17.5 %reduce-scatter.28.cloned.1.call-done = bf16[512,256]{1,0:T(8,128)(2,1)} async-done(((bf16[1024,256]{1,0:T(8,128)(2,1)}), bf16[512,256]{1,0:T(8,128)(2,1)}) %reduce-scatter.28.cloned.1.call-update) | async-done | bytes 262160 | tf_op jit(solution)/shard_map/reduce_scatter | solution.py:370
  1096.8 17.2 %reduce-scatter.26.cloned.1.call-done = bf16[512,256]{1,0:T(8,128)(2,1)} async-done(((bf16[1024,256]{1,0:T(8,128)(2,1)}), bf16[512,256]{1,0:T(8,128)(2,1)}) %reduce-scatter.26.cloned.1.call-update) | async-done | bytes 262160 | tf_op jit(solution)/shard_map/reduce_scatter | solution.py:367
  1128.7 118.1 %all-reduce.10.cloned.1.call-done = (bf16[512,704]{1,0:T(8,128)(2,1)}, bf16[512,704]{1,0:T(8,128)(2,1)}, bf16[512,256]{1,0:T(8,128)(2,1)}, bf16[512,256]{1,0:T(8...) async-done(((bf16[512,704]{1,0:T(8,128)(2,1)}, bf16[512,704]{1,0:T(8,128)(2,1)}, bf16[512,256]{1,0:T(8,128)(2,1)}, ...) | async-done | bytes 3211280 | tf_op jit(solution)/shard_map/psum | solution.py:406
  (292 shorter events, 360.4 us)
Async XLA Ops:
  8.1 40.0 %all-gather.12.cloned.1.call-start = ((), (), s32[]{:S(2)}) async-start(), calls=%async_computation.13 | async-start | bytes 3276800 | tf_op jit(solution)/shard_map/all_gather | solution.py:138
  17.7 94.0 %all-gather.14.cloned.1.call-start = ((), (), s32[]{:S(2)}) async-start(), calls=%async_computation.14 | async-start | bytes 3276800 | tf_op jit(solution)/shard_map/all_gather | solution.py:201
  55.2 113.1 %all-gather.16.cloned.1.call-start = ((), (), s32[]{:S(2)}) async-start(), calls=%async_computation.15 | async-start | bytes 3276800 | tf_op jit(solution)/shard_map/all_gather | solution.py:202
  56.0 344.0 %reduce-scatter.14.cloned.1.call-start = ((), (), s32[]{:S(2)}) async-start(), calls=%async_computation.16 | async-start | bytes 3276800 | tf_op jit(solution)/shard_map/reduce_scatter | solution.py:141
  209.0 196.4 %all-gather.20.cloned.1.call-start = ((), (), s32[]{:S(2)}) async-start(), calls=%async_computation.18 | async-start | bytes 2162688 | tf_op jit(solution)/shard_map/all_gather | solution.py:119
  209.6 210.2 %all-gather.22.cloned.1.call-start = ((), (), s32[]{:S(2)}) async-start(), calls=%async_computation.19 | async-start | bytes 2162688 | tf_op jit(solution)/shard_map/all_gather | solution.py:120
  210.2 237.1 %all-gather.18.cloned.1.call-start = ((), (), s32[]{:S(2)}) async-start(), calls=%async_computation.17 | async-start | bytes 3276800 | tf_op jit(solution)/shard_map/all_gather | solution.py:138
  214.6 342.0 %copy-start.30 = (f32[2,1,512]{2,1,0:T(1,128)}, f32[2,1,512]{2,1,0:T(1,128)S(1)}, u32[]{:S(2)}) copy-start(f32[2,1,512]{2,1,0:T(1,128)S(1)} %convert_element_type.378) | copy-start | bytes 12292
  403.6 70.9 %all-gather.24.cloned.1.call-start = ((), (), s32[]{:S(2)}) async-start(), calls=%async_computation.20 | async-start | bytes 2162688 | tf_op jit(solution)/shard_map/all_gather | solution.py:121
  404.4 97.3 %all-gather.26.cloned.1.call-start = ((), (), s32[]{:S(2)}) async-start(), calls=%async_computation.22 | async-start | bytes 3276800 | tf_op jit(solution)/shard_map/all_gather | solution.py:138
  405.1 149.2 %reduce-scatter.18.cloned.1.call-start = ((), (), s32[]{:S(2)}) async-start(), calls=%async_computation.23 | async-start | bytes 3276800 | tf_op jit(solution)/shard_map/reduce_scatter | solution.py:141
  519.6 65.2 %all-gather.28.cloned.1.call-start = ((), (), s32[]{:S(2)}) async-start(), calls=%async_computation.24 | async-start | bytes 3276800 | tf_op jit(solution)/shard_map/all_gather | solution.py:138
  559.1 347.6 %reduce-scatter.20.cloned.1.call-start = ((), (), s32[]{:S(2)}) async-start(), calls=%async_computation.25 | async-start | bytes 3276800 | tf_op jit(solution)/shard_map/reduce_scatter | solution.py:335
  688.8 272.0 %reduce-scatter.22.cloned.1.call-start = ((), (), s32[]{:S(2)}) async-start(), calls=%async_computation.26 | async-start | bytes 3276800 | tf_op jit(solution)/shard_map/reduce_scatter | solution.py:341
  691.8 296.2 %reduce-scatter.38.cloned.1.call-start = ((), (), s32[]{:S(2)}) async-start(), calls=%async_computation.34 | async-start | bytes 2162688 | tf_op jit(solution)/shard_map/reduce_scatter | solution.py:391
  697.3 319.0 %reduce-scatter.36.cloned.1.call-start = ((), (), s32[]{:S(2)}) async-start(), calls=%async_computation.33 | async-start | bytes 2359296 | tf_op jit(solution)/shard_map/reduce_scatter | solution.py:388
  708.2 336.4 %reduce-scatter.34.cloned.1.call-start = ((), (), s32[]{:S(2)}) async-start(), calls=%async_computation.32 | async-start | bytes 2359296 | tf_op jit(solution)/shard_map/reduce_scatter | solution.py:385
  708.8 353.3 %reduce-scatter.32.cloned.1.call-start = ((), (), s32[]{:S(2)}) async-start(), calls=%async_computation.31 | async-start | bytes 786432 | tf_op jit(solution)/shard_map/reduce_scatter | solution.py:382
  712.7 366.6 %reduce-scatter.30.cloned.1.call-start = ((), (), s32[]{:S(2)}) async-start(), calls=%async_computation.30 | async-start | bytes 786432 | tf_op jit(solution)/shard_map/reduce_scatter | solution.py:376
  966.2 130.6 %reduce-scatter.28.cloned.1.call-start = ((), (), s32[]{:S(2)}) async-start(), calls=%async_computation.29 | async-start | bytes 786432 | tf_op jit(solution)/shard_map/reduce_scatter | solution.py:370
  967.0 147.1 %reduce-scatter.26.cloned.1.call-start = ((), (), s32[]{:S(2)}) async-start(), calls=%async_computation.28 | async-start | bytes 786432 | tf_op jit(solution)/shard_map/reduce_scatter | solution.py:367
  967.5 279.2 %all-reduce.10.cloned.1.call-start = ((), (), s32[]{:S(2)}) async-start(), calls=%async_computation.35 | async-start | bytes 6684672 | tf_op jit(solution)/shard_map/psum | solution.py:406
  1114.1 145.1 %reduce-scatter.24.cloned.1.call-start = ((), (), s32[]{:S(2)}) async-start(), calls=%async_computation.27 | async-start | bytes 3276800 | tf_op jit(solution)/shard_map/reduce_scatter | solution.py:141
  1119.7 141.3 %reduce-scatter.16.cloned.1.call-start = ((), (), s32[]{:S(2)}) async-start(), calls=%async_computation.21 | async-start | bytes 3276800 | tf_op jit(solution)/shard_map/reduce_scatter | solution.py:141
  (46 other events, 1155.9 us)
Sparse Core Ops, SparseCore 0:
  17.8 27.3 all-gather.11
  55.3 56.2 all-gather.13
  113.8 53.5 all-gather.15
  209.1 190.7 reduce-scatter.13
  559.2 25.5 all-gather.27
  688.9 217.7 reduce-scatter.19
  909.0 51.7 reduce-scatter.21
  963.6 24.3 reduce-scatter.37
  990.3 26.0 reduce-scatter.35
  1018.5 26.0 reduce-scatter.33
  1047.5 14.5 reduce-scatter.31
  1064.8 14.5 reduce-scatter.29
  1082.2 14.5 reduce-scatter.27
  1099.5 14.5 reduce-scatter.25
  1117.1 129.5 all-reduce.9
Sparse Core Ops, SparseCore 1:
  211.0 181.7 all-gather.19
  394.2 25.5 all-gather.21
  421.9 25.4 all-gather.17
  448.9 25.5 all-gather.23
  476.2 25.4 all-gather.25
  519.7 34.6 reduce-scatter.17
  1119.7 34.6 reduce-scatter.23
  1157.0 34.6 reduce-scatter.15
where the time goes:
time: 1300 us; the launch traced here: 1290 us
  waiting for transfers between devices  889 us (68%)
  matrix products  171 us (13%)
  blocking collectives  59.4 us (5%)
  loops' own time  59.1 us (5%)
  other arithmetic  55 us (4%)
  local copies, waits for them, and re-layouts  41.5 us (3%)
  between operations  17.4 us (1%)
    reduce_scatter x4, waiting for transfers between devices, sum_rows(): lax.psum_scatter(jnp.einsum('rbk,dk->rbd', operand, weight, preferred_ele...  220 us
    reduce_scatter x1, waiting for transfers between devices, on_device(): lax.psum_scatter(jnp.stack(key_grad_trees, axis=1).astype(jnp.bfloat16),...  194 us
    psum x1, waiting for transfers between devices, on_device(): lax.psum(owned[4].astype(jnp.bfloat16), 'ctx').astype(jnp.float32)  118 us
    all_gather x4, waiting for transfers between devices, gather_rows(): return lax.all_gather(values, 'tp', axis=0, tiled=True)  77.5 us
    another operation x12, loops' own time, over_pieces(): running = lax.cond(piece_at <= ctx_place, visit_piece, keep_same, running)  59 us
    reduce_scatter x1, waiting for transfers between devices, on_device(): lax.psum_scatter(jnp.stack(value_grad_trees, axis=1).astype(jnp.bfloat16)...  51.6 us
    all_gather x1, waiting for transfers between devices, fetch_keys(): lax.all_gather(key_vectors, 'ctx', axis=0, tiled=True)  47.5 us
    reduce_scatter x1, waiting for transfers between devices, on_device(): lax.psum_scatter(grad_up.astype(jnp.bfloat16), 'fsdp', scatter_dimension=...  28.4 us
  transfers between devices with their start and end apart: 23, of which 18 were waited for; matrix products, arithmetic and copies ran while one was open for 10% of the time, Pallas kernels for 0%

commit v1 on v0

v1 whole, which is shorter than its diff:
```python
import functools
import math

import jax
import jax.numpy as jnp
from jax import lax
from jax.experimental import pallas as pl
from jax.experimental.pallas import tpu as pltpu
from jax.sharding import PartitionSpec as P

HEAD = 64
HALF = HEAD // 2
CHUNK = 128
BIG = 1e30
LOG2E = 1.4426950408889634
SCORE_SCALE = HEAD**-0.5
QUERY_SCALE = SCORE_SCALE * LOG2E
epsilon = 1e-05
f32 = jnp.float32
bf16 = jnp.bfloat16


def dot(a, b, ca, cb):
    return lax.dot_general(a, b, (((ca,), (cb,)), ((), ())), preferred_element_type=f32)


def layout_kernel(par_ref, len_ref, pos_ref, qx_ref, kx_ref, seg_ref, need_ref, anc_sc, above_sc, *, segs, tokens):
    token = lax.broadcasted_iota(jnp.int32, (1, tokens), 1)
    pos = jnp.zeros((1, tokens), jnp.int32)
    seg_of = jnp.full((1, tokens), -1, jnp.int32)
    bits = jnp.zeros((1, tokens), jnp.int32)
    for b in range(tokens // CHUNK):
        seg_ref[b] = 0
        need_ref[b] = 0
    off = jnp.int32(0)
    for s in range(segs):
        length = len_ref[0, s]
        if s == 0:
            anc, above = jnp.int32(1), jnp.int32(0)
        else:
            parent = par_ref[0, s]
            anc = anc_sc[parent] | jnp.int32(1 << s)
            above = above_sc[parent] + len_ref[0, parent]
        anc_sc[s] = anc
        above_sc[s] = above
        started = token >= off
        seg_of = jnp.where(started, s, seg_of)
        pos = jnp.where(started, token - off + above, pos)
        bits = jnp.where(started, anc, bits)

        def mark(b, carry, anc=anc, s=s):
            seg_ref[b] = seg_ref[b] | jnp.int32(1 << s)
            need_ref[b] = need_ref[b] | anc
            return carry

        lax.fori_loop(off // CHUNK, (off + length - 1) // CHUNK + 1, mark, 0)
        off = off + length
    pos_ref[...] = pos.astype(f32)
    row = lax.broadcasted_iota(jnp.int32, (kx_ref.shape[0], tokens), 0)
    kx_ref[...] = jnp.where(row == seg_of, -BIG, 0.0).astype(bf16)
    linked = lax.shift_right_logical(jnp.broadcast_to(bits, row.shape), row) & 1
    qx_ref[...] = jnp.where(linked == 1, 0.0, 1.0).astype(bf16)


SMEM = pl.BlockSpec(memory_space=pltpu.SMEM)
VMEM = pl.BlockSpec(memory_space=pltpu.VMEM)


def layout_call(parents, lengths, tokens):
    segs = parents.shape[-1]
    rows = -(-segs // 16) * 16
    return pl.pallas_call(
        functools.partial(layout_kernel, segs=segs, tokens=tokens),
        out_shape=(
            jax.ShapeDtypeStruct((1, tokens), f32),
            jax.ShapeDtypeStruct((rows, tokens), bf16),
            jax.ShapeDtypeStruct((rows, tokens), bf16),
            jax.ShapeDtypeStruct((tokens // CHUNK,), jnp.int32),
            jax.ShapeDtypeStruct((tokens // CHUNK,), jnp.int32),
        ),
        in_specs=[SMEM, SMEM],
        out_specs=(VMEM, VMEM, VMEM, SMEM, SMEM),
        scratch_shapes=[pltpu.SMEM((segs,), jnp.int32), pltpu.SMEM((segs,), jnp.int32)],
        cost_estimate=pl.CostEstimate(flops=0, bytes_accessed=1 << 20, transcendentals=0),
        name="layout",
    )(parents, lengths)


def any_bits(ref, first, count):
    bits = ref[first]
    for j in range(1, count):
        bits = bits | ref[first + j]
    return bits


def causal(scores, key_first, query_first):
    key_at = key_first + lax.broadcasted_iota(jnp.int32, scores.shape, 0)
    query_at = query_first + lax.broadcasted_iota(jnp.int32, scores.shape, 1)
    return jnp.where(key_at <= query_at, scores, -BIG)


def piece_place(place_ref, at):
    shift, half = divmod(at, 2)
    ctx = lax.rem(place_ref[0] - shift + place_ref[2], place_ref[2])
    return ctx * 2 + lax.rem(place_ref[1] + half, 2)


def chunks_at(ref, first, count):
    return jnp.concatenate([ref[first + j] for j in range(count)], axis=1)


def fwd_kernel(place_ref, seg_ref, need_ref, qx_ref, kx_ref, *rest, tile, pieces, extra):
    qkv_refs = rest[:pieces]
    out_ref, full_ref, lse_ref, keys, values, queries, top, total = rest[pieces:]
    at = pl.program_id(0)
    piece = qkv_refs[0].shape[1]
    per = piece // CHUNK
    pad = jnp.zeros((128 - HEAD - extra, CHUNK), bf16)

    @pl.when(at == 0)
    def _():
        for p in range(pieces):
            place = piece_place(place_ref, p)
            for c in range(per):
                g = place * per + c
                lanes = slice(c * CHUNK, (c + 1) * CHUNK)
                rows = pl.ds(pl.multiple_of(g * CHUNK, CHUNK), CHUNK)
                ref = qkv_refs[p]
                keys[rows, :] = jnp.concatenate([ref[HEAD : 2 * HEAD, lanes], kx_ref[:, rows], pad], axis=0).T
                values[g] = jnp.concatenate([ref[2 * HEAD :, lanes], jnp.ones((16, CHUNK), bf16)], axis=0)
                queries[g] = jnp.concatenate([ref[:HEAD, lanes], qx_ref[:, rows], pad], axis=0)

    per_tile = tile // CHUNK
    query = chunks_at(queries, at * per_tile, per_tile)
    need = any_bits(need_ref, at * per_tile, per_tile)

    def visit(key_at, diagonal):
        scores = dot(keys[pl.ds(pl.multiple_of(key_at * tile, tile), tile), :], query, 1, 0)
        value = chunks_at(values, key_at * per_tile, per_tile)
        if diagonal:
            scores = causal(scores, key_at * tile, at * tile)
            new_top = jnp.max(scores, axis=0, keepdims=True)
            weights = jnp.exp2(scores - new_top).astype(bf16)
            total[...] = dot(value, weights, 1, 0)
        else:
            old_top = top[...]
            new_top = jnp.maximum(old_top, jnp.max(scores, axis=0, keepdims=True))
            weights = jnp.exp2(scores - new_top).astype(bf16)
            total[...] = total[...] * jnp.exp2(old_top - new_top) + dot(value, weights, 1, 0)
        top[...] = new_top

    visit(at, True)

    def step(key_at, carry):
        @pl.when((any_bits(seg_ref, key_at * per_tile, per_tile) & need) != 0)
        def _():
            visit(key_at, False)

        return carry

    lax.fori_loop(0, at, step, 0)
    final = total[...]
    weight_sum = final[HEAD : HEAD + 1, :]
    mixed = final[:HEAD, :] * (1.0 / weight_sum)
    lse = top[...] + jnp.log2(weight_sum)
    for j in range(per_tile):
        g = at * per_tile + j
        lanes = slice(j * CHUNK, (j + 1) * CHUNK)
        out_ref[g // per, :, pl.ds(pl.multiple_of(lax.rem(g, per) * CHUNK, CHUNK), CHUNK)] = mixed[:, lanes].astype(bf16)
        full_ref[g] = mixed[:, lanes]
        lse_ref[g] = lse[:, lanes]


def fwd_call(place, seg, need, qx, kx, qkv, tile=512):
    pieces, piece = len(qkv), qkv[0].shape[1]
    tokens = pieces * piece
    chunks = tokens // CHUNK
    return pl.pallas_call(
        functools.partial(fwd_kernel, tile=tile, pieces=pieces, extra=qx.shape[0]),
        grid=(tokens // tile,),
        out_shape=(
            jax.ShapeDtypeStruct((pieces, HEAD, piece), bf16),
            jax.ShapeDtypeStruct((chunks, HEAD, CHUNK), f32),
            jax.ShapeDtypeStruct((chunks, 1, CHUNK), f32),
        ),
        in_specs=[SMEM, SMEM, SMEM] + [VMEM] * (2 + pieces),
        out_specs=(VMEM, VMEM, VMEM),
        scratch_shapes=[
            pltpu.VMEM((tokens, 128), bf16),
            pltpu.VMEM((chunks, HEAD + 16, CHUNK), bf16),
            pltpu.VMEM((chunks, 128, CHUNK), bf16),
            pltpu.VMEM((1, tile), f32),
            pltpu.VMEM((HEAD + 16, tile), f32),
        ],
        compiler_params=pltpu.CompilerParams(vmem_limit_bytes=40 << 20),
        cost_estimate=pl.CostEstimate(flops=tokens * tokens * HEAD * 4, bytes_accessed=8 << 20, transcendentals=tokens * tokens // 2),
        name="attend",
    )(place, seg, need, qx, kx, *qkv)


def three_parts(row):
    at = lax.broadcasted_iota(jnp.int32, (16, row.shape[1]), 0)
    high = row.astype(bf16).astype(f32)
    rest = row - high
    mid = rest.astype(bf16).astype(f32)
    low = rest - mid
    return jnp.where(at == 0, high, jnp.where(at == 1, mid, jnp.where(at == 2, low, 0.0))).astype(bf16)


def unrotate(values, cosine, sine):
    a, b = values[:HALF], values[HALF:]
    return jnp.concatenate([a * cosine + b * sine, b * cosine - a * sine], axis=0)


def bwd_kernel(place_ref, seg_ref, need_ref, qx_ref, kx_ref, full_ref, lse_ref, cos_ref, sin_ref, *rest, tile, pieces, extra):
    qkv_refs, grad_refs = rest[:pieces], rest[pieces : 2 * pieces]
    out_ref, keys, values, queries, grads, key_lanes, key_sum, value_sum, query_sum = rest[2 * pieces :]
    at = pl.program_id(0)
    piece = qkv_refs[0].shape[1]
    per = piece // CHUNK

    @pl.when(at == 0)
    def _():
        minus = jnp.full((16, CHUNK), -1.0, bf16)
        pad_key = jnp.zeros((128 - HEAD - extra - 16, CHUNK), bf16)
        pad_value = jnp.zeros((128 - HEAD - 16, CHUNK), bf16)
        for p in range(pieces):
            place = piece_place(place_ref, p)
            for c in range(per):
                g = place * per + c
                lanes = slice(c * CHUNK, (c + 1) * CHUNK)
                rows = pl.ds(pl.multiple_of(g * CHUNK, CHUNK), CHUNK)
                ref = qkv_refs[p]
                key = ref[HEAD : 2 * HEAD, lanes]
                grad = grad_refs[p][:, lanes]
                key_lanes[g] = key
                keys[rows, :] = jnp.concatenate([key, kx_ref[:, rows], minus, pad_key], axis=0).T
                values[rows, :] = jnp.concatenate([ref[2 * HEAD :, lanes], minus, pad_value], axis=0).T
                queries[g] = jnp.concatenate([ref[:HEAD, lanes], qx_ref[:, rows], three_parts(lse_ref[g]), pad_key], axis=0)
                delta = jnp.sum(grad.astype(f32) * full_ref[g], axis=0, keepdims=True)
                grads[g] = jnp.concatenate([grad, three_parts(delta), pad_value], axis=0)
        key_sum[...] = jnp.zeros(key_sum.shape, f32)
        value_sum[...] = jnp.zeros(value_sum.shape, f32)

    per_tile = tile // CHUNK
    query = chunks_at(queries, at * per_tile, per_tile)
    grad = chunks_at(grads, at * per_tile, per_tile)
    need = any_bits(need_ref, at * per_tile, per_tile)

    def visit(key_at, diagonal):
        rows = pl.ds(pl.multiple_of(key_at * tile, tile), tile)
        scores = dot(keys[rows, :], query, 1, 0)
        if diagonal:
            scores = causal(scores, key_at * tile, at * tile)
        probs = jnp.exp2(scores)
        prob_grad = dot(values[rows, :], grad, 1, 0)
        score_grad = (probs * prob_grad).astype(bf16)
        query_part = dot(chunks_at(key_lanes, key_at * per_tile, per_tile), score_grad, 1, 0)
        value_part = dot(grad[:HEAD], probs.astype(bf16), 1, 1)
        key_part = dot(query[:HEAD], score_grad, 1, 1)
        if diagonal:
            query_sum[...] = query_part
        else:
            query_sum[...] += query_part
        for j in range(per_tile):
            lanes = slice(j * CHUNK, (j + 1) * CHUNK)
            value_sum[key_at * per_tile + j] += value_part[:, lanes]
            key_sum[key_at * per_tile + j] += key_part[:, lanes]

    visit(at, True)

    def step(key_at, carry):
        @pl.when((any_bits(seg_ref, key_at * per_tile, per_tile) & need) != 0)
        def _():
            visit(key_at, False)

        return carry

    lax.fori_loop(0, at, step, 0)
    for j in range(per_tile):
        g = at * per_tile + j
        lanes = slice(j * CHUNK, (j + 1) * CHUNK)
        rows = pl.ds(pl.multiple_of(g * CHUNK, CHUNK), CHUNK)
        out_ref[g // per, :HEAD, pl.ds(pl.multiple_of(lax.rem(g, per) * CHUNK, CHUNK), CHUNK)] = unrotate(
            query_sum[:, lanes] * SCORE_SCALE, cos_ref[:, rows], sin_ref[:, rows]
        ).astype(bf16)

    @pl.when(at == pl.num_programs(0) - 1)
    def _():
        for p in range(pieces):
            for c in range(per):
                g = p * per + c
                lanes = slice(c * CHUNK, (c + 1) * CHUNK)
                rows = slice(g * CHUNK, (g + 1) * CHUNK)
                out_ref[p, HEAD : 2 * HEAD, lanes] = unrotate(
                    key_sum[g] * (1.0 / LOG2E), cos_ref[:, rows], sin_ref[:, rows]
                ).astype(bf16)
                out_ref[p, 2 * HEAD :, lanes] = (0.5 * value_sum[g]).astype(bf16)


def bwd_call(place, seg, need, qx, kx, full, lse, cosine, sine, qkv, grads, tile=512):
    pieces, piece = len(qkv), qkv[0].shape[1]
    tokens = pieces * piece
    chunks = tokens // CHUNK
    return pl.pallas_call(
        functools.partial(bwd_kernel, tile=tile, pieces=pieces, extra=qx.shape[0]),
        grid=(tokens // tile,),
        out_shape=jax.ShapeDtypeStruct((pieces, 3 * HEAD, piece), bf16),
        in_specs=[SMEM, SMEM, SMEM] + [VMEM] * (6 + 2 * pieces),
        out_specs=VMEM,
        scratch_shapes=[
            pltpu.VMEM((tokens, 128), bf16),
            pltpu.VMEM((tokens, 128), bf16),
            pltpu.VMEM((chunks, 128, CHUNK), bf16),
            pltpu.VMEM((chunks, 128, CHUNK), bf16),
            pltpu.VMEM((chunks, HEAD, CHUNK), bf16),
            pltpu.VMEM((chunks, HEAD, CHUNK), f32),
            pltpu.VMEM((chunks, HEAD, CHUNK), f32),
            pltpu.VMEM((HEAD, tile), f32),
        ],
        compiler_params=pltpu.CompilerParams(vmem_limit_bytes=48 << 20),
        cost_estimate=pl.CostEstimate(flops=tokens * tokens * HEAD * 8, bytes_accessed=12 << 20, transcendentals=tokens * tokens // 2),
        name="attend_back",
    )(place, seg, need, qx, kx, full, lse, cosine, sine, *qkv, *grads)


def on_device(
    tokens, first_values, cotangent, parents, seg_lengths,
    w_query, w_key, w_value, w_out, w_gate, w_up, w_down, gain_attn, gain_ffn,
):
    assert tokens.shape[1] == 1
    fsdp_count, ctx_count, tp_count = (lax.axis_size(a) for a in ("fsdp", "ctx", "tp"))
    assert tp_count == 4
    fsdp_at, ctx_at, tp_at = (lax.axis_index(a) for a in ("fsdp", "ctx", "tp"))
    core_at, x_at = tp_at % 2, tp_at // 2
    own_rows, width = tokens.shape[0], tokens.shape[2]
    chip_rows = 2 * own_rows
    heads = w_query.shape[1] // HEAD
    assert heads == ctx_count
    tree_len = own_rows * tp_count * ctx_count
    weight_rows = w_query.shape[0]

    def over_core(value):
        return lax.ppermute(value, "tp", [(i, i ^ 1) for i in range(tp_count)])

    def over_x(value):
        return lax.ppermute(value, "tp", [(i, i ^ 2) for i in range(tp_count)])

    def ctx_shift(value, shift):
        return lax.ppermute(value, "ctx", [(i, (i + shift) % ctx_count) for i in range(ctx_count)])

    def fsdp_shift(value, shift):
        return lax.ppermute(value, "fsdp", [(i, (i + shift) % fsdp_count) for i in range(fsdp_count)])

    def by_core(own, other):
        return jnp.where(core_at == 0, jnp.concatenate([own, other], axis=0), jnp.concatenate([other, own], axis=0))

    def full_rows(shard):
        if fsdp_count != 2:
            return lax.all_gather(shard, "fsdp", axis=0, tiled=True)
        size = shard.shape[0]
        whole = jnp.zeros((size * fsdp_count,) + shard.shape[1:], shard.dtype)
        whole = lax.dynamic_update_slice_in_dim(whole, shard, fsdp_at * size, 0)
        for shift in range(1, fsdp_count):
            source = (fsdp_at - shift) % fsdp_count
            whole = lax.dynamic_update_slice_in_dim(whole, fsdp_shift(shard, shift), source * size, 0)
        return whole

    def reduce_grad(partial):
        if fsdp_count != 2:
            low = lax.psum_scatter(partial.astype(bf16), "fsdp", scatter_dimension=0, tiled=True)
            return lax.psum(low, "ctx").astype(f32)
        total = lax.dynamic_slice_in_dim(partial, fsdp_at * weight_rows, weight_rows, 0)
        for shift in range(1, fsdp_count):
            target = (fsdp_at + shift) % fsdp_count
            piece = lax.dynamic_slice_in_dim(partial, target * weight_rows, weight_rows, 0).astype(bf16)
            total = total + fsdp_shift(piece, shift).astype(f32)
        if ctx_count != 4:
            return lax.psum(total.astype(bf16), "ctx").astype(f32)
        low = total.astype(bf16)
        low = (low.astype(f32) + lax.ppermute(low, "ctx", [(0, 1), (3, 2)]).astype(f32)).astype(bf16)
        low = (low.astype(f32) + lax.ppermute(low, "ctx", [(1, 2), (2, 1)]).astype(f32)).astype(bf16)
        back = lax.ppermute(low, "ctx", [(1, 0), (2, 3)])
        return jnp.where((ctx_at == 0) | (ctx_at == 3), back, low).astype(f32)

    own_tokens, own_cot = tokens[:, 0, :], cotangent[:, 0, :]
    token_core = over_core(own_tokens)
    token_x = over_x(own_tokens)
    attention_gain = full_rows(gain_attn.reshape(weight_rows, 1)).reshape(1, width).astype(f32)
    w_query, w_key, w_value = full_rows(w_query), full_rows(w_key), full_rows(w_value)
    token_x_core = over_core(token_x)
    qkv_weight = jnp.concatenate([w_query, w_key, w_value], axis=1)
    out_weight = full_rows(w_out)
    out_weight_x = over_x(out_weight)
    cot_core = over_core(own_cot)
    cot_x = over_x(own_cot)
    cot_x_core = over_core(cot_x)
    down_weight = full_rows(w_down)
    gate_weight = full_rows(w_gate)
    up_weight = full_rows(w_up)
    ffn_gain = full_rows(gain_ffn.reshape(weight_rows, 1)).reshape(1, width).astype(f32)

    place = jnp.stack([ctx_at, x_at, jnp.full_like(ctx_at, ctx_count)]).astype(jnp.int32)
    position, query_extra, key_extra, seg_bits, need_bits = layout_call(parents, seg_lengths, tree_len)
    frequency = jnp.exp(-math.log(10000.0) * jnp.arange(HALF, dtype=f32) / HALF)
    angles = frequency[:, None] * position
    cosine, sine = jnp.cos(angles), jnp.sin(angles)

    def normalize(rows_f32):
        return lax.rsqrt(jnp.mean(rows_f32 * rows_f32, axis=-1, keepdims=True) + epsilon)

    first_flat = first_values[:, 0, :]

    def project(rows, x_half):
        single = rows.astype(f32)
        unit = single * normalize(single)
        normed = (unit * attention_gain).astype(bf16)
        projected = dot(qkv_weight, normed, 0, 1).reshape(3, heads, HEAD, chip_rows)
        where_at = (ctx_at * 2 + x_half) * chip_rows
        cos_own = lax.dynamic_slice_in_dim(cosine, where_at, chip_rows, 1)
        sin_own = lax.dynamic_slice_in_dim(sine, where_at, chip_rows, 1)
        a, b = projected[:2, :, :HALF], projected[:2, :, HALF:]
        turned = jnp.concatenate([a * cos_own - b * sin_own, b * cos_own + a * sin_own], axis=2)
        first = lax.dynamic_slice_in_dim(first_flat, x_half * chip_rows, chip_rows, 0).T.reshape(heads, HEAD, chip_rows)
        value = 0.5 * projected[2] + 0.5 * first.astype(f32)
        joined = jnp.stack([turned[0] * QUERY_SCALE, turned[1], value], axis=1).astype(bf16)
        return joined.reshape(heads, 3 * HEAD, chip_rows), normed

    def head_exchange(by_head):
        received = []
        for shift in range(ctx_count):
            piece = lax.dynamic_index_in_dim(by_head, (ctx_at + shift) % ctx_count, 0, keepdims=False)
            received.append(ctx_shift(piece, shift) if shift else piece)
        return received

    chip_tokens = by_core(own_tokens, token_core)
    far_tokens = by_core(token_x, token_x_core)
    near_qkv, near_normed = project(chip_tokens, x_at)
    near_pieces = head_exchange(near_qkv)
    far_qkv, far_normed = project(far_tokens, 1 - x_at)
    far_pieces = head_exchange(far_qkv)
    qkv = [p for pair in zip(near_pieces, far_pieces) for p in pair]

    mixed_all, mixed_full, log_total = fwd_call(place, seg_bits, need_bits, query_extra, key_extra, qkv)

    def token_exchange(pieces, half, feature):
        buffer = jnp.zeros((feature // HEAD, heads, HEAD, chip_rows), bf16)
        for shift in range(ctx_count):
            target = (ctx_at + shift) % ctx_count
            piece = lax.dynamic_index_in_dim(pieces, target * 2 + half, 0, keepdims=False)
            got = ctx_shift(piece, shift) if shift else piece
            source = (ctx_at - shift) % ctx_count
            buffer = lax.dynamic_update_slice(
                buffer, got.reshape(feature // HEAD, 1, HEAD, chip_rows), (0, source, 0, 0)
            )
        return buffer.reshape(feature * heads, chip_rows)

    far_mixed = token_exchange(mixed_all, 1 - x_at, HEAD)
    far_mixed_recv = over_x(far_mixed)
    near_mixed = token_exchange(mixed_all, x_at, HEAD)

    middle_part = dot(near_mixed, out_weight, 0, 1) + dot(far_mixed_recv, out_weight_x, 0, 1)
    other_part = lax.dynamic_slice_in_dim(middle_part, (1 - core_at) * own_rows, own_rows, 0).astype(bf16)
    own_part = lax.dynamic_slice_in_dim(middle_part, core_at * own_rows, own_rows, 0)
    middle = own_tokens.astype(f32) + own_part + over_core(other_part).astype(f32)

    middle_scale = normalize(middle)
    ffn_own = (middle * middle_scale * ffn_gain).astype(bf16)
    ffn_core = over_core(ffn_own)
    ffn_x = over_x(ffn_own)
    ffn_x_core = over_core(ffn_x)

    def feed(rows, cot_rows):
        gate = dot(rows, gate_weight, 1, 0)
        up = dot(rows, up_weight, 1, 0)
        hidden_grad = dot(cot_rows, down_weight, 1, 0)
        sig = 1.0 / (1.0 + jnp.exp(-gate))
        act = gate * sig
        hidden = (act * up).astype(bf16)
        gate_grad = (hidden_grad * up * (sig * (1.0 + gate * (1.0 - sig)))).astype(bf16)
        up_grad = (hidden_grad * act).astype(bf16)
        result = dot(hidden, down_weight, 1, 1)
        back = dot(gate_grad, gate_weight, 1, 1) + dot(up_grad, up_weight, 1, 1)
        return hidden, gate_grad, up_grad, result, back

    near_ffn = jnp.concatenate([ffn_own, ffn_core], axis=0)
    far_ffn = jnp.concatenate([ffn_x, ffn_x_core], axis=0)
    near_cot = jnp.concatenate([own_cot, cot_core], axis=0)
    far_cot = jnp.concatenate([cot_x, cot_x_core], axis=0)
    near_hidden, near_gate, near_up, near_result, near_back = feed(near_ffn, near_cot)
    far_hidden, far_gate, far_up, far_result, far_back = feed(far_ffn, far_cot)

    def scatter_rows(near, far):
        far_sum = far[:own_rows] + over_core(far[own_rows:].astype(bf16)).astype(f32)
        near_sum = near[:own_rows] + over_core(near[own_rows:].astype(bf16)).astype(f32)
        return near_sum + over_x(far_sum.astype(bf16)).astype(f32)

    ffn_grad = scatter_rows(near_back, far_back)
    weighted = ffn_grad * ffn_gain
    middle_grad = (
        own_cot.astype(f32)
        + middle_scale * weighted
        - middle * (middle_scale**3 * jnp.mean(weighted * middle, axis=-1, keepdims=True))
    )
    ffn_gain_part = jnp.sum(ffn_grad * middle * middle_scale, axis=0)
    middle_low = middle_grad.astype(bf16)
    low_core = over_core(middle_low)
    chip_low = by_core(middle_low, low_core)
    far_heads = dot(out_weight_x, chip_low, 0, 1).astype(bf16)
    far_out_grad = over_x(far_heads).reshape(heads, HEAD, chip_rows)
    near_out_grad = dot(out_weight, chip_low, 0, 1).astype(bf16).reshape(heads, HEAD, chip_rows)
    near_grads = head_exchange(near_out_grad)
    far_grads = head_exchange(far_out_grad)
    grads = [p for pair in zip(near_grads, far_grads) for p in pair]

    layer_out = (middle + scatter_rows(near_result, far_result)).astype(bf16)
    grad_down = reduce_grad(dot(near_cot, near_hidden, 0, 0) + dot(far_cot, far_hidden, 0, 0))
    grad_gate = reduce_grad(dot(near_ffn, near_gate, 0, 0) + dot(far_ffn, far_gate, 0, 0))
    grad_up = reduce_grad(dot(near_ffn, near_up, 0, 0) + dot(far_ffn, far_up, 0, 0))
    low_x = over_x(middle_low)
    far_low = by_core(low_x, over_core(low_x))
    grad_out = reduce_grad(dot(chip_low, near_mixed, 0, 1) + dot(far_low, far_mixed, 0, 1))

    back_all = bwd_call(
        place, seg_bits, need_bits, query_extra, key_extra, mixed_full, log_total, cosine, sine, qkv, grads
    )
    far_projected = token_exchange(back_all, 1 - x_at, 3 * HEAD)
    near_projected = token_exchange(back_all, x_at, 3 * HEAD)

    far_normed_grad = dot(far_projected, qkv_weight, 0, 1)
    near_normed_grad = dot(near_projected, qkv_weight, 0, 1)

    def split_core(rows):
        mine = lax.dynamic_slice_in_dim(rows, core_at * own_rows, own_rows, 0)
        other = lax.dynamic_slice_in_dim(rows, (1 - core_at) * own_rows, own_rows, 0)
        return mine, other.astype(bf16)

    far_mine, far_other = split_core(far_normed_grad)
    far_sum = (far_mine + over_core(far_other).astype(f32)).astype(bf16)
    near_mine, near_other = split_core(near_normed_grad)
    normed_grad = near_mine + over_core(near_other).astype(f32) + over_x(far_sum).astype(f32)

    single = own_tokens.astype(f32)
    scale = normalize(single)
    weighted = normed_grad * attention_gain
    grad_tokens = (
        middle_grad + scale * weighted - single * (scale**3 * jnp.mean(weighted * single, axis=-1, keepdims=True))
    )
    attention_gain_part = jnp.sum(normed_grad * single * scale, axis=0)

    grad_qkv = dot(near_normed, near_projected, 0, 1) + dot(far_normed, far_projected, 0, 1)
    head_width = heads * HEAD
    grad_query = reduce_grad(grad_qkv[:, :head_width])
    grad_key = reduce_grad(grad_qkv[:, head_width : 2 * head_width])
    grad_value = reduce_grad(grad_qkv[:, 2 * head_width :])

    gains = lax.psum(jnp.stack([attention_gain_part, ffn_gain_part]), ("fsdp", "ctx", "tp"))
    gains = lax.dynamic_slice_in_dim(gains, fsdp_at * weight_rows, weight_rows, 1)

    near_value = near_projected[2 * head_width :].T.astype(f32)
    far_value = far_projected[2 * head_width :].T.astype(f32)
    grad_values = jnp.where(
        x_at == 0, jnp.concatenate([near_value, far_value], axis=0), jnp.concatenate([far_value, near_value], axis=0)
    )
    return (
        layer_out[:, None, :],
        grad_tokens[:, None, :],
        grad_values[:, None, :],
        grad_query,
        grad_key,
        grad_value,
        grad_out,
        grad_gate,
        grad_up,
        grad_down,
        gains[0],
        gains[1],
    )


def solution(mesh):
    rows, columns = P(("ctx", "tp"), "fsdp", None), P("ctx", "fsdp", "tp")
    weight, gain = P("fsdp", "tp"), P("fsdp")
    return jax.shard_map(
        on_device,
        mesh=mesh,
        in_specs=(rows, columns, rows, P("fsdp", None), P("fsdp", None)) + (weight,) * 7 + (gain,) * 2,
        out_specs=(rows, rows, columns) + (weight,) * 7 + (gain,) * 2,
        check_vma=False,
    )
```

time: 1300 us -> 583 us (0.45)
  waiting for transfers between devices: 889 us -> 205 us
  starting transfers between devices: 1.62 us -> 126 us
  matrix products: 171 us -> 56 us
  Pallas kernels: 0 us -> 83.5 us
  loops' own time: 59.1 us -> 0 us
  other arithmetic: 55 us -> 30.9 us
  blocking collectives: 59.4 us -> 37.3 us
  between operations: 17.4 us -> 3.19 us
    reduce_scatter x13 -> x0, waiting for transfers between devices: 612 us -> none  [the longest x4 220 us: sum_rows(): lax.psum_scatter(jnp.einsum('rbk,dk->rbd', operand, weight, preferred_ele...]
    ppermute x0 -> x86, waiting for transfers between devices: none -> 205 us  [the longest x24 67.9 us: ctx_shift(): lax.ppermute(value, 'ctx', [(i, (i + shift) % ctx_count) for i in range(c...]
    all_gather x9 -> x0, waiting for transfers between devices: 154 us -> none  [the longest x4 77.5 us: gather_rows(): return lax.all_gather(values, 'tp', axis=0, tiled=True)]
    ppermute x0 -> x86, starting transfers between devices: none -> 126 us  [the longest x24 62.1 us: ctx_shift(): lax.ppermute(value, 'ctx', [(i, (i + shift) % ctx_count) for i in range(c...]
    psum x1 -> x0, waiting for transfers between devices: 118 us -> none  [on_device(): lax.psum(owned[4].astype(jnp.bfloat16), 'ctx').astype(jnp.float32)]
    dot_general x39 -> x30, matrix products: 171 us -> 56 us  [dot(): lax.dot_general(a, b, (((ca,), (cb,)), ((), ())), preferred_element_type=...]
    pallas_call x0 -> x3, Pallas kernels: none -> 83.5 us  [the longest x1 48.8 us: bwd_call(): pl.pallas_call(functools.partial(bwd_kernel, tile=tile, pieces=pieces, ex...]
    another operation x13 -> x0, loops' own time: 59.1 us -> none  [the longest x12 59 us: over_pieces(): running = lax.cond(piece_at <= ctx_place, visit_piece, keep_same, running)]
  transfers between devices with their start and end apart: 23 -> 86, of which waited for: 18 -> 34; matrix products, arithmetic and copies ran while one was open for 10% -> 19% of each run, Pallas kernels for 0% -> 15%
where the time goes in v1:
time: 583 us; the launch traced here: 573 us
  waiting for transfers between devices  205 us (35%)
  starting transfers between devices  126 us (22%)
  Pallas kernels  83.5 us (14%)
  matrix products  56 us (10%)
  blocking collectives  37.3 us (6%)
  other arithmetic  30.9 us (5%)
  local copies, waits for them, and re-layouts  30.7 us (5%)
    ppermute x24, waiting for transfers between devices, ctx_shift(): lax.ppermute(value, 'ctx', [(i, (i + shift) % ctx_count) for i in range(c...  67.9 us
    ppermute x24, starting transfers between devices, ctx_shift(): lax.ppermute(value, 'ctx', [(i, (i + shift) % ctx_count) for i in range(c...  62.1 us
    ppermute x16, waiting for transfers between devices, fsdp_shift(): lax.ppermute(value, 'fsdp', [(i, (i + shift) % fsdp_count) for i in range...  58.2 us
    dot_general x30, matrix products, dot(): lax.dot_general(a, b, (((ca,), (cb,)), ((), ())), preferred_element_type=...  56 us
    pallas_call x1, Pallas kernels, bwd_call(): pl.pallas_call(functools.partial(bwd_kernel, tile=tile, pieces=pieces, ex...  48.8 us
    ppermute x7, waiting for transfers between devices, reduce_grad(): lax.ppermute(low, 'ctx', [(0, 1), (3, 2)]).astype(f32)  45.2 us
    psum x1, blocking collectives, on_device(): lax.psum(jnp.stack([attention_gain_part, ffn_gain_part]), ('fsdp', 'ctx',...  37.3 us
    pallas_call x1, Pallas kernels, fwd_call(): pl.pallas_call(functools.partial(fwd_kernel, tile=tile, pieces=pieces, ex...  31.9 us
  transfers between devices with their start and end apart: 86, of which 34 were waited for; matrix products, arithmetic and copies ran while one was open for 19% of the time, Pallas kernels for 15%

profile of v1, /device:TPU:0, one launch (start us, length us, event | category | flops | bytes accessed | tf_op | source)
XLA Modules:
  0.0 573.4 jit_solution(11859687798405347514)
XLA Ops:
  60.1 5.4 collective-permute-done.9.rest_4_
  72.4 14.0 %collective-permute-done.10.rest_5_ = bf16[192,640]{1,0:T(8,128)(2,1)S(1)} collective-permute-done((bf16[192,640]{1,0:T(8,128)(2,1)S(1)}, bf16[192,640]{1,0:T(8,128)(2,1)S(1)}, u32[]{:S(2)}, u32[]{:S(2)}) %collective-permute-start.10) | collective-permute-done | bytes 245792 | tf_op jit(solution)/shard_map/ppermute | solution.py:350
  86.4 31.9 %attend.1 = (bf16[8,64,640]{2,1,0:T(8,128)(2,1)S(1)}, f32[40,64,128]{2,1,0:T(8,128)S(1)}, f32[40,1,128]{2,1,0:T(1,128)S(1)}) custom-call(s32[3]{0:T(128)S(1)} %pad_add_fusion.place_ref, s32[40]{0:T(128)S(1)} %copy-done.2, s32[40]{0:T(128)S(1)} %copy-done.3, bf16[16,5120]{1,0:T(8,128)(2,1)S(1)} %copy-done, bf16[16,5120]{1,0:T(8,128)(2,1)S(1)} %copy-done.1, ...), custom_call_target="tpu_custom_call" | custom-call | flops 6710886400 | bytes 8388608 | tf_op jit(solution)/shard_map/attend/pallas_call | solution.py:178
  118.4 5.8 %collective-permute-start.17 = (bf16[64,640]{1,0:T(8,128)(2,1)S(1)}, bf16[64,640]{1,0:T(8,128)(2,1)S(1)}, u32[]{:S(2)}, u32[]{:S(2)}) collective-permute-start(bf16[64,640]{1,0:T(8,128)(2,1)S(1)} %get-tuple-element.95), channel_id=1, source_target_pairs={{0,4},{4,8},{8,12},{12,0},{1,5},{5,9},{9,13},{13,1},{2,6},{6,10},{... | collective-permute-start | bytes 245768 | tf_op jit(solution)/shard_map/ppermute | solution.py:350
  129.5 5.1 collective-permute-done.13
  135.5 5.0 collective-permute-done.19
  151.0 6.7 %collective-permute-done.25 = bf16[512,704]{0,1:T(8,128)(2,1)S(1)} collective-permute-done((bf16[512,704]{0,1:T(8,128)(2,1)S(1)}, bf16[512,704]{0,1:T(8,128)(2,1)S(1)}, u32[]{:S(2)}, u32[]{:S(2)}) %collective-permute-start.25) | collective-permute-done | bytes 720928 | tf_op jit(solution)/shard_map/ppermute | solution.py:353
  172.2 6.3 %collective-permute-done.29 = bf16[320,1024]{1,0:T(8,128)(2,1)S(1)} collective-permute-done((bf16[320,1024]{1,0:T(8,128)(2,1)S(1)}, bf16[320,1024]{1,0:T(8,128)(2,1)S(1)}, u32[]{:S(2)}, u32[]{:S(2)}) %collective-permute-start.29) | collective-permute-done | bytes 655392 | tf_op jit(solution)/shard_map/ppermute | solution.py:347
  179.9 9.6 %fusion.27 = f32[1024,704]{0,1:T(8,128)S(1)} fusion(bf16[640,704]{0,1:T(8,128)(2,1)S(1)} %get-tuple-element.63, bf16[320,1024]{1,0:T(8,128)(2,1)S(1)} %collective-permute-done.33, bf16[320,1024]{1,0:T(8,128)(2,1)S(1)} %bitcast.229), kind=kOutput, calls=%fused_computation.100 | convolution fusion | flops 925368320 | bytes 5095424 | tf_op jit(solution)/shard_map/dot_general | solution.py:24
  206.3 11.7 %collective-permute-done.74 = bf16[512,704]{0,1:T(8,128)(2,1)S(1)} collective-permute-done((bf16[512,704]{0,1:T(8,128)(2,1)S(1)}, bf16[512,704]{0,1:T(8,128)(2,1)S(1)}, u32[]{:S(2)}, u32[]{:S(2)}) %collective-permute-start.74) | collective-permute-done | bytes 720928 | tf_op jit(solution)/shard_map/ppermute | solution.py:353
  219.7 13.6 %collective-permute-done.78 = bf16[512,704]{0,1:T(8,128)(2,1)S(1)} collective-permute-done((bf16[512,704]{0,1:T(8,128)(2,1)S(1)}, bf16[512,704]{0,1:T(8,128)(2,1)S(1)}, u32[]{:S(2)}, u32[]{:S(2)}) %collective-permute-start.78) | collective-permute-done | bytes 720928 | tf_op jit(solution)/shard_map/ppermute | solution.py:353
  235.2 13.2 %collective-permute-done.82 = bf16[512,704]{0,1:T(8,128)(2,1)S(1)} collective-permute-done((bf16[512,704]{0,1:T(8,128)(2,1)S(1)}, bf16[512,704]{0,1:T(8,128)(2,1)S(1)}, u32[]{:S(2)}, u32[]{:S(2)}) %collective-permute-start.82) | collective-permute-done | bytes 720928 | tf_op jit(solution)/shard_map/ppermute | solution.py:353
  258.0 9.3 %collective-permute-done.75 = bf16[512,704]{0,1:T(8,128)(2,1)S(1)} collective-permute-done((bf16[512,704]{0,1:T(8,128)(2,1)S(1)}, bf16[512,704]{0,1:T(8,128)(2,1)S(1)}, u32[]{:S(2)}, u32[]{:S(2)}) %collective-permute-start.75) | collective-permute-done | bytes 720928 | tf_op jit(solution)/shard_map/ppermute | solution.py:381
  268.3 14.5 %collective-permute-done.79 = bf16[512,704]{0,1:T(8,128)(2,1)S(1)} collective-permute-done((bf16[512,704]{0,1:T(8,128)(2,1)S(1)}, bf16[512,704]{0,1:T(8,128)(2,1)S(1)}, u32[]{:S(2)}, u32[]{:S(2)}) %collective-permute-start.79) | collective-permute-done | bytes 720928 | tf_op jit(solution)/shard_map/ppermute | solution.py:381
  283.8 13.1 %collective-permute-done.83 = bf16[512,704]{0,1:T(8,128)(2,1)S(1)} collective-permute-done((bf16[512,704]{0,1:T(8,128)(2,1)S(1)}, bf16[512,704]{0,1:T(8,128)(2,1)S(1)}, u32[]{:S(2)}, u32[]{:S(2)}) %collective-permute-start.83) | collective-permute-done | bytes 720928 | tf_op jit(solution)/shard_map/ppermute | solution.py:381
  319.8 48.8 %attend_back.1 = bf16[8,192,640]{2,1,0:T(8,128)(2,1)} custom-call(s32[3]{0:T(128)S(1)} %pad_add_fusion.place_ref, s32[40]{0:T(128)S(1)} %copy-done.2, s32[40]{0:T(128)S(1)} %copy-done.3, bf16[16,5120]{1,0:T(8,128)(2,1)S(1)} %copy-done, bf16[16,5120]{1,0:T(8,128)(2,1)S(1)} %copy-done.1, f32[40,64,128]{2,1,0:T(8,128)S(1)} %get-tuple-element.26.full_ref, ...), custom_call_target="tpu_custom_call" | custom-call | flops 13421772800 | bytes 12582912 | tf_op jit(solution)/shard_map/attend_back/pallas_call | solution.py:305
  379.2 11.4 %collective-permute-start.47 = (bf16[192,640]{1,0:T(8,128)(2,1)S(1)}, bf16[192,640]{1,0:T(8,128)(2,1)S(1)}, u32[]{:S(2)}, u32[]{:S(2)}) collective-permute-start(bf16[192,640]{1,0:T(8,128)(2,1)S(1)} %get-tuple-element.80), channel_id=1, source_target_pairs={{0,4},{4,8},{8,12},{12,0},{1,5},{5,9},{9,13},{13,1},{2,6},{6,10},{... | collective-permute-start | bytes 737288 | tf_op jit(solution)/shard_map/ppermute | solution.py:350
  394.4 10.5 %collective-permute-start.48 = (bf16[192,640]{1,0:T(8,128)(2,1)S(1)}, bf16[192,640]{1,0:T(8,128)(2,1)S(1)}, u32[]{:S(2)}, u32[]{:S(2)}) collective-permute-start(bf16[192,640]{1,0:T(8,128)(2,1)S(1)} %get-tuple-element.79), channel_id=1, source_target_pairs={{0,8},{4,12},{8,0},{12,4},{1,9},{5,13},{9,1},{13,5},{2,10},{6,14},... | collective-permute-start | bytes 737288 | tf_op jit(solution)/shard_map/ppermute | solution.py:350
  407.5 6.2 %collective-permute-done.48 = bf16[192,640]{1,0:T(8,128)(2,1)S(1)} collective-permute-done((bf16[192,640]{1,0:T(8,128)(2,1)S(1)}, bf16[192,640]{1,0:T(8,128)(2,1)S(1)}, u32[]{:S(2)}, u32[]{:S(2)}) %collective-permute-start.48) | collective-permute-done | bytes 245792 | tf_op jit(solution)/shard_map/ppermute | solution.py:350
  417.5 20.1 %collective-permute-done.49 = bf16[192,640]{1,0:T(8,128)(2,1)S(1)} collective-permute-done((bf16[192,640]{1,0:T(8,128)(2,1)S(1)}, bf16[192,640]{1,0:T(8,128)(2,1)S(1)}, u32[]{:S(2)}, u32[]{:S(2)}) %collective-permute-start.49) | collective-permute-done | bytes 245792 | tf_op jit(solution)/shard_map/ppermute | solution.py:350
  486.3 4.2 collective-permute-done.65
  503.8 11.3 %collective-permute-done.59 = bf16[512,256]{1,0:T(8,128)(2,1)S(1)} collective-permute-done((bf16[512,256]{1,0:T(8,128)(2,1)S(1)}, bf16[512,256]{1,0:T(8,128)(2,1)S(1)}, u32[]{:S(2)}, u32[]{:S(2)}) %collective-permute-start.59) | collective-permute-done | bytes 262176 | tf_op jit(solution)/shard_map/ppermute | solution.py:383
  521.6 4.8 collective-permute-done.67
  535.0 37.3 %psum.7 = f32[2,1024]{1,0:T(2,128)S(1)} all-reduce(f32[2,1024]{1,0:T(2,128)S(1)} %pad_maximum_fusion.9), channel_id=1, replica_groups=mesh['fsdp'=2,'ctx'=4,'tp'=4] {'fsdp','ctx','tp'}, use_global_device_ids=true, to_apply=%region_8.9 | all-reduce | flops 2048 | bytes 16384 | tf_op jit(solution)/shard_map/psum | solution.py:557
  (437 shorter events, 250.3 us)
Async XLA Ops:
  4.3 30.6 %collective-permute-start.3 = (bf16[320,1024]{1,0:T(8,128)(2,1)}, bf16[320,1024]{1,0:T(8,128)(2,1)}, u32[]{:S(2)}, u32[]{:S(2)}) collective-permute-start(bf16[320,1024]{1,0:T(8,128)(2,1)} %bitcast.207), channel_id=1, source_target_pairs={{0,1},{1,0},{2,3},{3,2},{4,5},{5,4},{6,7},{7,6},{8,9},{9,8},{10,11... | collective-permute-start | bytes 1966088 | tf_op jit(solution)/shard_map/ppermute | solution.py:344
  56.8 29.6 %collective-permute-start.10 = (bf16[192,640]{1,0:T(8,128)(2,1)S(1)}, bf16[192,640]{1,0:T(8,128)(2,1)S(1)}, u32[]{:S(2)}, u32[]{:S(2)}) collective-permute-start(bf16[192,640]{1,0:T(8,128)(2,1)S(1)} %get-tuple-element.84), channel_id=1, source_target_pairs={{0,8},{4,12},{8,0},{12,4},{1,9},{5,13},{9,1},{13,5},{2,10},{6,14},... | collective-permute-start | bytes 737288 | tf_op jit(solution)/shard_map/ppermute | solution.py:350
  65.5 84.1 %collective-permute-start.27 = (bf16[512,704]{0,1:T(8,128)(2,1)S(1)}, bf16[512,704]{0,1:T(8,128)(2,1)S(1)}, u32[]{:S(2)}, u32[]{:S(2)}) collective-permute-start(bf16[512,704]{0,1:T(8,128)(2,1)S(1)} %copy-done.24), channel_id=1, source_target_pairs={{0,16},{16,0},{1,17},{17,1},{2,18},{18,2},{3,19},{19,3},{4,20},{20... | collective-permute-start | bytes 2162696 | tf_op jit(solution)/shard_map/ppermute | solution.py:353
  67.2 83.2 %collective-permute-start.26 = (bf16[512,704]{0,1:T(8,128)(2,1)S(1)}, bf16[512,704]{0,1:T(8,128)(2,1)S(1)}, u32[]{:S(2)}, u32[]{:S(2)}) collective-permute-start(bf16[512,704]{0,1:T(8,128)(2,1)S(1)} %copy-done.26), channel_id=1, source_target_pairs={{0,16},{16,0},{1,17},{17,1},{2,18},{18,2},{3,19},{19,3},{4,20},{20... | collective-permute-start | bytes 2162696 | tf_op jit(solution)/shard_map/ppermute | solution.py:353
  70.8 76.2 %collective-permute-start.21 = (bf16[1024,256]{1,0:T(8,128)(2,1)S(1)}, bf16[1024,256]{1,0:T(8,128)(2,1)S(1)}, u32[]{:S(2)}, u32[]{:S(2)}) collective-permute-start(bf16[1024,256]{1,0:T(8,128)(2,1)S(1)} %constant_dynamic-update-slice_fusion.14), channel_id=1, source_target_pairs={{0,2},{1,3},{2,0},{3,1},{4,6},{5,7},{6,4},{7,5},{8,10},{9,11},{10,... | collective-permute-start | bytes 1572872 | tf_op jit(solution)/shard_map/ppermute | solution.py:347
  168.9 82.2 %collective-permute-start.34 = (bf16[320,1024]{1,0:T(8,128)(2,1)S(1)}, bf16[320,1024]{1,0:T(8,128)(2,1)S(1)}, u32[]{:S(2)}, u32[]{:S(2)}) collective-permute-start(bf16[320,1024]{1,0:T(8,128)(2,1)S(1)} %slice.208), channel_id=1, source_target_pairs={{0,1},{1,0},{2,3},{3,2},{4,5},{5,4},{6,7},{7,6},{8,9},{9,8},{10,11... | collective-permute-start | bytes 1966088 | tf_op jit(solution)/shard_map/ppermute | solution.py:344
  170.5 84.5 %collective-permute-start.28 = (bf16[320,1024]{1,0:T(8,128)(2,1)S(1)}, bf16[320,1024]{1,0:T(8,128)(2,1)S(1)}, u32[]{:S(2)}, u32[]{:S(2)}) collective-permute-start(bf16[320,1024]{1,0:T(8,128)(2,1)S(1)} %slice.210), channel_id=1, source_target_pairs={{0,1},{1,0},{2,3},{3,2},{4,5},{5,4},{6,7},{7,6},{8,9},{9,8},{10,11... | collective-permute-start | bytes 1966088 | tf_op jit(solution)/shard_map/ppermute | solution.py:344
  203.6 29.8 %collective-permute-start.78 = (bf16[512,704]{0,1:T(8,128)(2,1)S(1)}, bf16[512,704]{0,1:T(8,128)(2,1)S(1)}, u32[]{:S(2)}, u32[]{:S(2)}) collective-permute-start(bf16[512,704]{0,1:T(8,128)(2,1)S(1)} %dynamic-slice_convert_fusion.1), channel_id=1, source_target_pairs={{0,16},{16,0},{1,17},{17,1},{2,18},{18,2},{3,19},{19,3},{4,20},{20... | collective-permute-start | bytes 2162696 | tf_op jit(solution)/shard_map/ppermute | solution.py:353
  204.2 44.2 %collective-permute-start.82 = (bf16[512,704]{0,1:T(8,128)(2,1)S(1)}, bf16[512,704]{0,1:T(8,128)(2,1)S(1)}, u32[]{:S(2)}, u32[]{:S(2)}) collective-permute-start(bf16[512,704]{0,1:T(8,128)(2,1)S(1)} %dynamic-slice_convert_fusion), channel_id=1, source_target_pairs={{0,16},{16,0},{1,17},{17,1},{2,18},{18,2},{3,19},{19,3},{4,20},{20... | collective-permute-start | bytes 2162696 | tf_op jit(solution)/shard_map/ppermute | solution.py:353
  217.9 34.5 %collective-permute-start.38 = (bf16[320,1024]{1,0:T(8,128)(2,1)S(1)}, bf16[320,1024]{1,0:T(8,128)(2,1)S(1)}, u32[]{:S(2)}, u32[]{:S(2)}) collective-permute-start(bf16[320,1024]{1,0:T(8,128)(2,1)S(1)} %fusion.15), channel_id=1, source_target_pairs={{0,2},{1,3},{2,0},{3,1},{4,6},{5,7},{6,4},{7,5},{8,10},{9,11},{10,... | collective-permute-start | bytes 1966088 | tf_op jit(solution)/shard_map/ppermute | solution.py:347
  251.1 31.7 %collective-permute-start.79 = (bf16[512,704]{0,1:T(8,128)(2,1)S(1)}, bf16[512,704]{0,1:T(8,128)(2,1)S(1)}, u32[]{:S(2)}, u32[]{:S(2)}) collective-permute-start(bf16[512,704]{0,1:T(8,128)(2,1)S(1)} %add_convert_fusion.5), channel_id=1, source_target_pairs={{0,4},{12,8},{1,5},{13,9},{2,6},{14,10},{3,7},{15,11},{16,20},{28,... | collective-permute-start | bytes 2162696 | tf_op jit(solution)/shard_map/ppermute | solution.py:381
  252.5 44.5 %collective-permute-start.83 = (bf16[512,704]{0,1:T(8,128)(2,1)S(1)}, bf16[512,704]{0,1:T(8,128)(2,1)S(1)}, u32[]{:S(2)}, u32[]{:S(2)}) collective-permute-start(bf16[512,704]{0,1:T(8,128)(2,1)S(1)} %add_convert_fusion.2), channel_id=1, source_target_pairs={{0,4},{12,8},{1,5},{13,9},{2,6},{14,10},{3,7},{15,11},{16,20},{28,... | collective-permute-start | bytes 2162696 | tf_op jit(solution)/shard_map/ppermute | solution.py:381
  256.7 40.5 %collective-permute-start.39 = (bf16[320,1024]{1,0:T(8,128)(2,1)S(1)}, bf16[320,1024]{1,0:T(8,128)(2,1)S(1)}, u32[]{:S(2)}, u32[]{:S(2)}) collective-permute-start(bf16[320,1024]{1,0:T(8,128)(2,1)S(1)} %get-tuple-element.57), channel_id=1, source_target_pairs={{0,1},{1,0},{2,3},{3,2},{4,5},{5,4},{6,7},{7,6},{8,9},{9,8},{10,11... | collective-permute-start | bytes 1966088 | tf_op jit(solution)/shard_map/ppermute | solution.py:344
  256.7 53.7 %collective-permute-start.68 = (bf16[320,1024]{1,0:T(8,128)(2,1)S(1)}, bf16[320,1024]{1,0:T(8,128)(2,1)S(1)}, u32[]{:S(2)}, u32[]{:S(2)}) collective-permute-start(bf16[320,1024]{1,0:T(8,128)(2,1)S(1)} %get-tuple-element.57), channel_id=1, source_target_pairs={{0,2},{1,3},{2,0},{3,1},{4,6},{5,7},{6,4},{7,5},{8,10},{9,11},{10,... | collective-permute-start | bytes 1966088 | tf_op jit(solution)/shard_map/ppermute | solution.py:347
  267.5 35.9 %collective-permute-start.76 = (bf16[512,704]{0,1:T(8,128)(2,1)S(1)}, bf16[512,704]{0,1:T(8,128)(2,1)S(1)}, u32[]{:S(2)}, u32[]{:S(2)}) collective-permute-start(bf16[512,704]{0,1:T(8,128)(2,1)S(1)} %add_convert_fusion.7), channel_id=1, source_target_pairs={{4,8},{8,4},{5,9},{9,5},{6,10},{10,6},{7,11},{11,7},{20,24},{24,20... | collective-permute-start | bytes 2162696 | tf_op jit(solution)/shard_map/ppermute | solution.py:382
  283.0 30.5 %collective-permute-start.80 = (bf16[512,704]{0,1:T(8,128)(2,1)S(1)}, bf16[512,704]{0,1:T(8,128)(2,1)S(1)}, u32[]{:S(2)}, u32[]{:S(2)}) collective-permute-start(bf16[512,704]{0,1:T(8,128)(2,1)S(1)} %add_convert_fusion.4), channel_id=1, source_target_pairs={{4,8},{8,4},{5,9},{9,5},{6,10},{10,6},{7,11},{11,7},{20,24},{24,20... | collective-permute-start | bytes 2162696 | tf_op jit(solution)/shard_map/ppermute | solution.py:382
  315.5 57.3 %collective-permute-start.84 = (bf16[512,704]{0,1:T(8,128)(2,1)S(1)}, bf16[512,704]{0,1:T(8,128)(2,1)S(1)}, u32[]{:S(2)}, u32[]{:S(2)}) collective-permute-start(bf16[512,704]{0,1:T(8,128)(2,1)S(1)} %add_convert_fusion.1), channel_id=1, source_target_pairs={{4,8},{8,4},{5,9},{9,5},{6,10},{10,6},{7,11},{11,7},{20,24},{24,20... | collective-permute-start | bytes 2162696 | tf_op jit(solution)/shard_map/ppermute | solution.py:382
  316.2 132.4 %collective-permute-start.69 = (bf16[320,1024]{1,0:T(8,128)(2,1)S(1)}, bf16[320,1024]{1,0:T(8,128)(2,1)S(1)}, u32[]{:S(2)}, u32[]{:S(2)}) collective-permute-start(bf16[320,1024]{1,0:T(8,128)(2,1)S(1)} %collective-permute-done.68), channel_id=1, source_target_pairs={{0,1},{1,0},{2,3},{3,2},{4,5},{5,4},{6,7},{7,6},{8,9},{9,8},{10,11... | collective-permute-start | bytes 1966088 | tf_op jit(solution)/shard_map/ppermute | solution.py:344
  317.4 138.4 %collective-permute-start.77 = (bf16[512,704]{0,1:T(8,128)(2,1)}, bf16[512,704]{0,1:T(8,128)(2,1)}, u32[]{:S(2)}, u32[]{:S(2)}) collective-permute-start(bf16[512,704]{0,1:T(8,128)(2,1)} %add_convert_fusion.6), channel_id=1, source_target_pairs={{4,0},{8,12},{5,1},{9,13},{6,2},{10,14},{7,3},{11,15},{20,16},{24,... | collective-permute-start | bytes 2162696 | tf_op jit(solution)/shard_map/ppermute | solution.py:383
  390.7 70.0 %collective-permute-start.81 = (bf16[512,704]{0,1:T(8,128)(2,1)}, bf16[512,704]{0,1:T(8,128)(2,1)}, u32[]{:S(2)}, u32[]{:S(2)}) collective-permute-start(bf16[512,704]{0,1:T(8,128)(2,1)} %add_convert_fusion.3), channel_id=1, source_target_pairs={{4,0},{8,12},{5,1},{9,13},{6,2},{10,14},{7,3},{11,15},{20,16},{24,... | collective-permute-start | bytes 2162696 | tf_op jit(solution)/shard_map/ppermute | solution.py:383
  392.1 71.0 %collective-permute-start.85 = (bf16[512,704]{0,1:T(8,128)(2,1)}, bf16[512,704]{0,1:T(8,128)(2,1)}, u32[]{:S(2)}, u32[]{:S(2)}) collective-permute-start(bf16[512,704]{0,1:T(8,128)(2,1)} %add_convert_fusion), channel_id=1, source_target_pairs={{4,0},{8,12},{5,1},{9,13},{6,2},{10,14},{7,3},{11,15},{20,16},{24,... | collective-permute-start | bytes 2162696 | tf_op jit(solution)/shard_map/ppermute | solution.py:383
  437.6 58.4 %collective-permute-start.54 = (bf16[320,1024]{1,0:T(8,128)(2,1)}, bf16[320,1024]{1,0:T(8,128)(2,1)}, u32[]{:S(2)}, u32[]{:S(2)}) collective-permute-start(bf16[320,1024]{1,0:T(8,128)(2,1)} %dynamic-slice_convert_fusion.3), channel_id=1, source_target_pairs={{0,1},{1,0},{2,3},{3,2},{4,5},{5,4},{6,7},{7,6},{8,9},{9,8},{10,11... | collective-permute-start | bytes 1966088 | tf_op jit(solution)/shard_map/ppermute | solution.py:344
  448.6 81.9 %collective-permute-start.50 = (bf16[320,1024]{1,0:T(8,128)(2,1)}, bf16[320,1024]{1,0:T(8,128)(2,1)}, u32[]{:S(2)}, u32[]{:S(2)}) collective-permute-start(bf16[320,1024]{1,0:T(8,128)(2,1)} %dynamic-slice_convert_fusion.4), channel_id=1, source_target_pairs={{0,1},{1,0},{2,3},{3,2},{4,5},{5,4},{6,7},{7,6},{8,9},{9,8},{10,11... | collective-permute-start | bytes 1966088 | tf_op jit(solution)/shard_map/ppermute | solution.py:344
  498.0 32.4 %collective-permute-start.55 = (bf16[320,1024]{1,0:T(8,128)(2,1)S(1)}, bf16[320,1024]{1,0:T(8,128)(2,1)S(1)}, u32[]{:S(2)}, u32[]{:S(2)}) collective-permute-start(bf16[320,1024]{1,0:T(8,128)(2,1)S(1)} %add_convert_fusion.9), channel_id=1, source_target_pairs={{0,2},{1,3},{2,0},{3,1},{4,6},{5,7},{6,4},{7,5},{8,10},{9,11},{10,... | collective-permute-start | bytes 1966088 | tf_op jit(solution)/shard_map/ppermute | solution.py:347
  (114 other events, 1380.5 us)

commit v2 on v1

v2 whole, which is shorter than its diff:
```python
import functools
import math

import jax
import jax.numpy as jnp
from jax import lax
from jax.experimental import pallas as pl
from jax.experimental.pallas import tpu as pltpu
from jax.sharding import PartitionSpec as P

HEAD = 64
HALF = HEAD // 2
BIG = 1e30
LOG2E = 1.4426950408889634
SCORE_SCALE = HEAD**-0.5
QUERY_SCALE = SCORE_SCALE * LOG2E
epsilon = 1e-05
f32 = jnp.float32
bf16 = jnp.bfloat16


def dot(a, b, ca, cb):
    return lax.dot_general(a, b, (((ca,), (cb,)), ((), ())), preferred_element_type=f32)


def layout_kernel(par_ref, len_ref, pos_ref, qx_ref, kx_ref, seg_ref, need_ref, anc_sc, above_sc, *, segs, tokens, piece):
    token = lax.broadcasted_iota(jnp.int32, (1, tokens), 1)
    pos = jnp.zeros((1, tokens), jnp.int32)
    seg_of = jnp.full((1, tokens), -1, jnp.int32)
    bits = jnp.zeros((1, tokens), jnp.int32)
    for b in range(tokens // piece):
        seg_ref[b] = 0
        need_ref[b] = 0
    off = jnp.int32(0)
    for s in range(segs):
        length = len_ref[0, s]
        if s == 0:
            anc, above = jnp.int32(1), jnp.int32(0)
        else:
            parent = par_ref[0, s]
            anc = anc_sc[parent] | jnp.int32(1 << s)
            above = above_sc[parent] + len_ref[0, parent]
        anc_sc[s] = anc
        above_sc[s] = above
        started = token >= off
        seg_of = jnp.where(started, s, seg_of)
        pos = jnp.where(started, token - off + above, pos)
        bits = jnp.where(started, anc, bits)

        def mark(b, carry, anc=anc, s=s):
            seg_ref[b] = seg_ref[b] | jnp.int32(1 << s)
            need_ref[b] = need_ref[b] | anc
            return carry

        lax.fori_loop(off // piece, (off + length - 1) // piece + 1, mark, 0)
        off = off + length
    row = lax.broadcasted_iota(jnp.int32, (kx_ref.shape[1], tokens), 0)
    key_extra = jnp.where(row == seg_of, -BIG, 0.0).astype(bf16)
    linked = lax.shift_right_logical(jnp.broadcast_to(bits, row.shape), row) & 1
    query_extra = jnp.where(linked == 1, 0.0, 1.0).astype(bf16)
    for p in range(tokens // piece):
        lanes = slice(p * piece, (p + 1) * piece)
        pos_ref[p] = pos[:, lanes].astype(f32)
        kx_ref[p] = key_extra[:, lanes]
        qx_ref[p] = query_extra[:, lanes]


SMEM = pl.BlockSpec(memory_space=pltpu.SMEM)
VMEM = pl.BlockSpec(memory_space=pltpu.VMEM)


def layout_call(parents, lengths, tokens, piece):
    segs = parents.shape[-1]
    rows = -(-segs // 16) * 16
    return pl.pallas_call(
        functools.partial(layout_kernel, segs=segs, tokens=tokens, piece=piece),
        out_shape=(
            jax.ShapeDtypeStruct((tokens // piece, 1, piece), f32),
            jax.ShapeDtypeStruct((tokens // piece, rows, piece), bf16),
            jax.ShapeDtypeStruct((tokens // piece, rows, piece), bf16),
            jax.ShapeDtypeStruct((tokens // piece,), jnp.int32),
            jax.ShapeDtypeStruct((tokens // piece,), jnp.int32),
        ),
        in_specs=[SMEM, SMEM],
        out_specs=(VMEM, VMEM, VMEM, SMEM, SMEM),
        scratch_shapes=[pltpu.SMEM((segs,), jnp.int32), pltpu.SMEM((segs,), jnp.int32)],
        cost_estimate=pl.CostEstimate(flops=0, bytes_accessed=1 << 16, transcendentals=0),
        name="layout",
    )(parents, lengths)


def causal(scores):
    key_at = lax.broadcasted_iota(jnp.int32, scores.shape, 0)
    query_at = lax.broadcasted_iota(jnp.int32, scores.shape, 1)
    return jnp.where(key_at <= query_at, scores, -BIG)


def three_parts(row):
    at = lax.broadcasted_iota(jnp.int32, (16, row.shape[1]), 0)
    high = row.astype(bf16).astype(f32)
    rest = row - high
    mid = rest.astype(bf16).astype(f32)
    low = rest - mid
    return jnp.where(at == 0, high, jnp.where(at == 1, mid, jnp.where(at == 2, low, 0.0))).astype(bf16)


def unrotate(values, cosine, sine):
    a, b = values[:HALF], values[HALF:]
    return jnp.concatenate([a * cosine + b * sine, b * cosine - a * sine], axis=0)


def prep_kernel(place_ref, qx_ref, kx_ref, got_ref, keys, key_lanes, value_lanes, values, queries):
    piece = got_ref.shape[2] // 2
    extra = qx_ref.shape[1]
    minus = jnp.full((16, piece), -1.0, bf16)
    pad_key = jnp.zeros((128 - HEAD - extra - 16, piece), bf16)
    pad_value = jnp.zeros((128 - HEAD - 16, piece), bf16)
    for half in (0, 1):
        for p in range(got_ref.shape[0]):
            at = 2 * p + (place_ref[0] ^ half)
            got = got_ref[p, :, half * piece : (half + 1) * piece]
            query, key, value = got[:HEAD, :], got[HEAD : 2 * HEAD, :], got[2 * HEAD :, :]
            key_lanes[at] = key
            keys[at] = jnp.concatenate([key, kx_ref[at], minus, pad_key], axis=0).T
            value_lanes[at] = jnp.concatenate([value, -minus], axis=0)
            values[at] = jnp.concatenate([value, minus, pad_value], axis=0).T
            queries[at] = jnp.concatenate([query, qx_ref[at], jnp.zeros((128 - HEAD - extra, piece), bf16)], axis=0)


def shape_of(*sizes, dtype=bf16):
    return jax.ShapeDtypeStruct(sizes, dtype)


def call(kernel, name, out_shape, operands, scratch=(), scalars=1, mib=20, late=()):
    outs = out_shape if isinstance(out_shape, tuple) else (out_shape,)
    arrays = operands[scalars:]
    count, total = len(arrays), len(arrays) + len(outs)

    def body(*refs):
        first, rest = refs[:scalars], refs[scalars:]
        outside, inside, sems, rest = rest[:total], rest[total : 2 * total], rest[2 * total], rest[2 * total + 1 :]
        copies = [pltpu.make_async_copy(outside[i], inside[i], sems.at[i]) for i in range(count)]
        for copy in copies:
            copy.start()
        for i in range(count):
            if i not in late:
                copies[i].wait()
        more = {"ready": lambda: [copies[i].wait() for i in late]} if late else {}
        kernel(*first, *inside, *rest, **more)
        copies = [pltpu.make_async_copy(inside[i], outside[i], sems.at[i]) for i in range(count, total)]
        for copy in copies:
            copy.start()
        for copy in copies:
            copy.wait()

    got = pl.pallas_call(
        body,
        out_shape=outs,
        in_specs=[SMEM] * scalars + [pl.BlockSpec(memory_space=pltpu.HBM)] * count,
        out_specs=(pl.BlockSpec(memory_space=pltpu.HBM),) * len(outs),
        scratch_shapes=[pltpu.VMEM(x.shape, x.dtype) for x in (*arrays, *outs)]
        + [pltpu.SemaphoreType.DMA((total,))]
        + list(scratch),
        compiler_params=pltpu.CompilerParams(vmem_limit_bytes=60 << 20),
        cost_estimate=pl.CostEstimate(flops=0, bytes_accessed=1 << 16, transcendentals=0),
        name=name,
    )(*operands)
    return got if isinstance(out_shape, tuple) else got[0]


def prep_call(place, qx, kx, got):
    pieces, piece = 2 * got.shape[0], got.shape[2] // 2
    return call(
        prep_kernel,
        "prepare",
        (
            shape_of(pieces, piece, 128),
            shape_of(pieces, HEAD, piece),
            shape_of(pieces, HEAD + 16, piece),
            shape_of(pieces, piece, 128),
            shape_of(pieces, 128, piece),
        ),
        (place, qx, kx, got),
    )


def norm_kernel(place_ref, own_ref, other_ref, gain_ref, out_ref, *, swap):
    rows, width = own_ref.shape
    for half, ref in enumerate((own_ref, other_ref)):
        single = ref[...].astype(f32)
        scale = lax.rsqrt(jnp.mean(single * single, axis=-1, keepdims=True) + epsilon)
        if swap:
            turned = jnp.concatenate([single[:, width // 2 :], single[:, : width // 2]], axis=1)
            single = jnp.where(place_ref[3] == 0, single, turned)
        at = pl.multiple_of((place_ref[1] ^ half) * rows, rows)
        out_ref[pl.ds(at, rows), :] = (single * scale * gain_ref[...]).astype(bf16)


def norm_call(place, own, other, gain, swap):
    return call(
        functools.partial(norm_kernel, swap=swap), "normalise", shape_of(2 * own.shape[0], own.shape[1]),
        (place, own, other, gain), mib=16,
    )


def cut(ref, count):
    size = ref.shape[1] // count
    return [ref[:, i * size : (i + 1) * size] for i in range(count)]


def project_kernel(place_ref, near_ref, far_ref, cos_ref, sin_ref, first_ref, *rest, count):
    weights, (out, raw) = rest[:count], rest[count:]
    width = raw.shape[0] // 3
    size = near_ref.shape[1] // count
    piece = near_ref.shape[0]
    turned = [[w[i * size : (i + 1) * size, :].T for w in weights] for i in range(3)]
    for half, rows_ref in enumerate((near_ref, far_ref)):
        rows = cut(rows_ref, count)
        for i in range(3):
            raw[i * width : (i + 1) * width, :] = sum(dot(w, r, 1, 1) for w, r in zip(turned[i], rows))
        x_half = place_ref[0] ^ half
        at = 2 * place_ref[2] + x_half
        cosine, sine = cos_ref[at], sin_ref[at]
        start = pl.multiple_of(x_half * piece, piece)
        first = first_ref[pl.ds(start, piece), :].astype(f32).T

        def turn(values):
            a, b = values[:HALF], values[HALF:]
            return jnp.concatenate([a * cosine - b * sine, b * cosine + a * sine], axis=0)

        lanes = slice(half * piece, (half + 1) * piece)
        for at in range(width // HEAD):
            rows_at = [slice(i * width + at * HEAD, i * width + (at + 1) * HEAD) for i in range(3)]
            value = 0.5 * raw[rows_at[2], :] + 0.5 * first[at * HEAD : (at + 1) * HEAD]
            out[at, :HEAD, lanes] = (turn(raw[rows_at[0], :]) * QUERY_SCALE).astype(bf16)
            out[at, HEAD : 2 * HEAD, lanes] = turn(raw[rows_at[1], :]).astype(bf16)
            out[at, 2 * HEAD :, lanes] = value.astype(bf16)


def project_call(place, near, far, cosine, sine, first, weights):
    piece, width = near.shape[0], weights[0].shape[1]
    return call(
        functools.partial(project_kernel, count=len(weights)), "project",
        shape_of(width // HEAD, 3 * HEAD, 2 * piece),
        (place, near, far, cosine, sine, first, *weights),
        scratch=[pltpu.VMEM((3 * width, piece), f32)],
    )


def stack_kernel(*refs):
    out, at = refs[-1], 0
    for ref in refs[:-1]:
        rows = ref.shape[0]
        out[at : at + rows, :] = ref[...]
        at += rows


def pick_kernel(*refs):
    out = refs[-1]
    rows = out.shape[0]
    size = out.shape[1] // (len(refs) - 1)
    for i, ref in enumerate(refs[:-1]):
        out[:, i * size : (i + 1) * size] = ref[ref.shape[0] - rows :, :]


def pick_call(blocks, rows):
    return call(pick_kernel, "pick", shape_of(rows, blocks[0].shape[1] * len(blocks)), tuple(blocks), scalars=0)


def stack_call(*arrays):
    rows = sum(a.shape[0] for a in arrays)
    return call(stack_kernel, "stack", shape_of(rows, arrays[0].shape[1]), arrays, scalars=0, mib=16)


def split_core(place_ref, total, mine_ref, other_ref):
    rows = mine_ref.shape[0]
    mine_ref[...] = total[pl.ds(pl.multiple_of(place_ref[1] * rows, rows), rows), :]
    other_ref[...] = total[pl.ds(pl.multiple_of((1 - place_ref[1]) * rows, rows), rows), :].astype(bf16)


def output_kernel(place_ref, near_ref, far_ref, *rest):
    near_weight, far_weight, mine_ref, other_ref, total = rest
    total[...] = dot(near_ref[...].T, near_weight[...], 1, 0) + dot(far_ref[...].T, far_weight[...], 1, 0)
    split_core(place_ref, total, mine_ref, other_ref)


def output_call(place, near, far, near_weight, far_weight):
    rows, width = near.shape[1], near_weight.shape[1]
    return call(
        output_kernel, "out_project",
        (shape_of(rows // 2, width, dtype=f32), shape_of(rows // 2, width)),
        (place, near, far, near_weight, far_weight),
        scratch=[pltpu.VMEM((rows, width), f32)],
    )


def heads_kernel(place_ref, own_ref, other_ref, near_weight, far_weight, near_out, far_out, chip):
    rows = own_ref.shape[0]
    for half, ref in enumerate((own_ref, other_ref)):
        chip[pl.ds(pl.multiple_of((place_ref[1] ^ half) * rows, rows), rows), :] = ref[...]
    far_out[...] = dot(far_weight[...], chip[...], 1, 1).astype(bf16)
    near_out[...] = dot(near_weight[...], chip[...], 1, 1).astype(bf16)


def heads_call(place, own, other, near_weight, far_weight):
    rows, columns = 2 * own.shape[0], near_weight.shape[0]
    return call(
        heads_kernel, "out_back",
        (shape_of(columns, rows), shape_of(columns, rows), shape_of(rows, own.shape[1])),
        (place, own, other, near_weight, far_weight),
    )


def feed_kernel(rows_ref, other_ref, cot_ref, cot_other_ref, *rest, count):
    hidden = rest[count].shape[2]
    gate_w, up_w, down_w = ([w.at[i * hidden : (i + 1) * hidden] for w in rest[:count]] for i in range(3))
    hidden_ref, gate_ref, up_ref, mine_ref, sent_ref, rows_sc, cot_sc, back_sc = rest[count:]
    size = rows_ref.shape[0]
    rows_sc[0], rows_sc[1] = rows_ref[...], other_ref[...]
    cot_sc[0], cot_sc[1] = cot_ref[...], cot_other_ref[...]
    block = rows_ref.shape[1] // count

    def step(at, carry):
        lanes = [slice(i * block, (i + 1) * block) for i in range(count)]
        rows, cots = [rows_sc[at, :, s] for s in lanes], [cot_sc[at, :, s] for s in lanes]
        gate = sum(dot(r, w[...], 1, 1) for r, w in zip(rows, gate_w))
        up = sum(dot(r, w[...], 1, 1) for r, w in zip(rows, up_w))
        hidden_grad = sum(dot(r, w[...], 1, 1) for r, w in zip(cots, down_w))
        sig = 1.0 / (1.0 + jnp.exp(-gate))
        act = gate * sig
        hidden_ref[at] = (act * up).astype(bf16)
        gate_grad = (hidden_grad * up * (sig * (1.0 + gate * (1.0 - sig)))).astype(bf16)
        up_grad = (hidden_grad * act).astype(bf16)
        gate_ref[at] = gate_grad
        up_ref[at] = up_grad
        for i in range(count):
            back_sc[at, :, lanes[i]] = dot(gate_grad, gate_w[i][...], 1, 0) + dot(up_grad, up_w[i][...], 1, 0)
        return carry

    lax.fori_loop(0, 2, step, 0)
    mine_ref[...] = back_sc[0]
    sent_ref[...] = back_sc[1].astype(bf16)


def feed_call(rows, other, cot, cot_other, weights, hidden):
    size, width = rows.shape
    count = len(weights)
    return call(
        functools.partial(feed_kernel, count=count), "feed",
        (shape_of(2, size, hidden),) * 3 + (shape_of(size, width, dtype=f32), shape_of(size, width)),
        (rows, other, cot, cot_other, *weights),
        scratch=[pltpu.VMEM((2, size, width), bf16)] * 2 + [pltpu.VMEM((2, size, width), f32)],
        scalars=0, mib=40,
    )


def prep_back_kernel(place_ref, queries, near_grad, far_grad, near_full, far_full, near_lse, far_lse, queries_out, grads_out, *, extra):
    places, _, piece = near_grad.shape
    queries_out[...] = queries[...]
    pad = jnp.zeros((128 - HEAD - 16, piece), bf16)
    for half, (grad, full, lse) in enumerate(((near_grad, near_full, near_lse), (far_grad, far_full, far_lse))):
        for p in range(places):
            at = 2 * p + (place_ref[0] ^ half)
            queries_out[at, HEAD + extra : HEAD + extra + 16, :] = lse[p]
            delta = jnp.sum(grad[p].astype(f32) * full[p], axis=0, keepdims=True)
            grads_out[at] = jnp.concatenate([grad[p], three_parts(delta), pad], axis=0)


def prep_back_call(place, queries, extra, *rest):
    return call(
        functools.partial(prep_back_kernel, extra=extra), "prepare_back",
        (shape_of(*queries.shape), shape_of(*queries.shape)), (place, queries, *rest), mib=16,
    )


def weights_kernel(near_rows, far_rows, far_kv, last, *rest, count):
    width = near_rows.shape[1] // count
    columns = far_kv.shape[0] * HEAD
    flat = lambda ref, at: ref[:, at * HEAD : (at + 1) * HEAD, :].reshape(columns, ref.shape[2])
    pairs = ((flat(last, 2), flat(last, 3)), (flat(last, 0), flat(far_kv, 0)), (flat(last, 1), flat(far_kv, 1)))
    for i, (near, far) in enumerate(pairs):
        for b in range(count):
            lanes = slice(b * width, (b + 1) * width)
            total = dot(near, near_rows[:, lanes], 1, 0) + dot(far, far_rows[:, lanes], 1, 0)
            rest[b][i * width : (i + 1) * width, :] = total.T.astype(bf16)


def weights_call(near_rows, far_rows, far_kv, last, count):
    width, columns = near_rows.shape[1] // count, far_kv.shape[0] * HEAD
    return call(
        functools.partial(weights_kernel, count=count), "weight_grads",
        tuple(shape_of(3 * width, columns) for _ in range(count)),
        (near_rows, far_rows, far_kv, last), scalars=0,
    )


def rows_kernel(place_ref, rows_ref, kv, last, *rest, half, count):
    weights, (mine_ref, other_ref, gain_ref, total) = rest[:count], rest[count:]
    columns = kv.shape[0] * HEAD
    flat = lambda ref, at: ref[:, at * HEAD : (at + 1) * HEAD, :].reshape(columns, ref.shape[2])
    if half:
        grads = flat(last, 3), flat(kv, 0), flat(kv, 1)
    else:
        grads = flat(last, 2), flat(last, 0), flat(last, 1)
    grads = [g.T for g in grads]
    size = total.shape[1] // count
    for i in range(count):
        part = sum(dot(g, weights[i][j * size : (j + 1) * size, :], 1, 1) for j, g in enumerate(grads))
        lanes = slice(i * size, (i + 1) * size)
        total[:, lanes] = part
        gain_ref[:, lanes] = jnp.sum(part * rows_ref[:, lanes].astype(f32), axis=0, keepdims=True)
    split_core(place_ref, total, mine_ref, other_ref)


def rows_call(place, rows, kv, last, weights, half):
    size, width = rows.shape
    return call(
        functools.partial(rows_kernel, half=half, count=len(weights)), "rows_back",
        (shape_of(size // 2, width, dtype=f32), shape_of(size // 2, width), shape_of(1, width, dtype=f32)),
        (place, rows, kv, last, *weights),
        scratch=[pltpu.VMEM((size, width), f32)],
    )


def feed_grads_kernel(near_gate, far_gate, near_up, far_up, near_hidden, far_hidden, *refs):
    rows, cots, outs = refs[:4], refs[4:8], refs[8:]
    count = len(outs) // 2
    size = rows[0].shape[1] // count
    hidden = near_gate.shape[2]
    pairs = ((near_gate, far_gate, rows), (near_up, far_up, rows), (near_hidden, far_hidden, cots))
    for b in range(count):
        lanes = slice(b * size, (b + 1) * size)
        for i, (near, far, right) in enumerate(pairs):
            near, far = (ref[...].reshape(2 * ref.shape[1], hidden) for ref in (near, far))
            near_right, far_right = (jnp.concatenate([right[j][:, lanes], right[j + 1][:, lanes]], axis=0) for j in (0, 2))
            total = (dot(near, near_right, 0, 0) + dot(far, far_right, 0, 0)).astype(bf16)
            if i < 2:
                outs[b][i * hidden : (i + 1) * hidden, :] = total
            else:
                outs[count + b][...] = total


def feed_grads_call(lefts, hiddens, rows, cots, count):
    hidden, size = lefts[0].shape[2], rows[0].shape[1] // count
    outs = call(
        feed_grads_kernel, "feed_grads",
        (shape_of(2 * hidden, size),) * count + (shape_of(hidden, size),) * count,
        (*lefts, *hiddens, *rows, *cots), scalars=0, mib=40,
    )
    return outs[:count], outs[count:]


def result_kernel(near_hidden, far_hidden, *rest, count):
    weights, (near_mine, far_mine, sent) = rest[:count], rest[count:]
    size = near_mine.shape[1] // count
    for at, (ref, mine) in enumerate(((near_hidden, near_mine), (far_hidden, far_mine))):
        for i in range(count):
            lanes = slice(i * size, (i + 1) * size)
            weight = weights[i][2 * ref.shape[2] : 3 * ref.shape[2], :]
            mine[:, lanes] = dot(ref[0], weight, 1, 0)
            sent[at, :, lanes] = dot(ref[1], weight, 1, 0).astype(bf16)


def result_call(near_hidden, far_hidden, weights):
    _, size, _ = near_hidden.shape
    count = len(weights)
    width = weights[0].shape[1] * count
    return call(
        functools.partial(result_kernel, count=count), "result",
        (shape_of(size, width, dtype=f32), shape_of(size, width, dtype=f32), shape_of(2, size, width)),
        (near_hidden, far_hidden, *weights), scalars=0, mib=24,
    )


def out_grads_kernel(place_ref, chip_low, far_own, far_other, near_mixed, far_mixed, *rest):
    outs, far_low = rest[:-1], rest[-1]
    count = len(outs)
    rows = far_own.shape[0]
    for half, ref in enumerate((far_own, far_other)):
        far_low[pl.ds(pl.multiple_of((place_ref[1] ^ half) * rows, rows), rows), :] = ref[...]
    near, far = near_mixed[...], far_mixed[...]
    for out, near_rows, far_rows in zip(outs, cut(chip_low, count), cut(far_low, count)):
        out[...] = (dot(near, near_rows, 1, 0) + dot(far, far_rows, 1, 0)).T.astype(bf16)


def out_grads_call(place, chip_low, far_own, far_other, near_mixed, far_mixed, count):
    width, columns = chip_low.shape[1] // count, near_mixed.shape[0]
    return call(
        out_grads_kernel, "out_grads", tuple(shape_of(width, columns) for _ in range(count)),
        (place, chip_low, far_own, far_other, near_mixed, far_mixed),
        scratch=[pltpu.VMEM(chip_low.shape, bf16)],
    )


def join_kernel(*refs):
    count = len(refs) // 3
    for i in range(count):
        a, b, out = refs[2 * i], refs[2 * i + 1], refs[2 * count + i]
        out[...] = (a[...].astype(f32) + b[...].astype(f32)).astype(bf16)


def join_call(*pairs):
    outs = call(
        join_kernel, "join", tuple(shape_of(*a.shape) for a, _ in pairs), [x for pair in pairs for x in pair],
        scalars=0, mib=16,
    )
    return list(outs)


def collect(first, last, hit, todo):
    def step(at, count):
        todo[count] = at
        return count + hit(at).astype(jnp.int32)

    return lax.fori_loop(first, last, step, jnp.int32(0))


def two_ahead(count, todo, first, fill, work):
    def step(j, now):
        middle, after = todo[2 * j], todo[2 * j + 1]
        fill(1, middle)
        work(0, now)
        fill(0, after)
        work(1, middle)
        return after

    last = lax.fori_loop(0, count // 2, step, first)

    @pl.when(lax.rem(count, 2) == 0)
    def _():
        work(0, last)

    @pl.when(lax.rem(count, 2) == 1)
    def _():
        final = todo[count - 1]
        fill(1, final)
        work(0, last)
        work(1, final)


def fwd_kernel(todo_ref, seg_ref, need_ref, keys, values, queries, out_ref, full_ref, lse_ref, score_a, score_b, top, total, todo):
    scores = (score_a, score_b)

    def attend(i, carry):
        at = todo_ref[i]
        need = need_ref[at]
        count = collect(0, at, lambda k: (seg_ref[k] & need) != 0, todo)
        query = queries[at]
        score_a[...] = causal(dot(keys[at], query, 1, 0))
        top[...] = jnp.full(top.shape, -BIG, f32)
        total[...] = jnp.zeros(total.shape, f32)

        def fill(slot, key_at):
            scores[slot][...] = dot(keys[key_at], query, 1, 0)

        def work(slot, key_at):
            score = scores[slot][...]
            old_top = top[...]
            new_top = jnp.maximum(old_top, jnp.max(score, axis=0, keepdims=True))
            weights = jnp.exp2(score - new_top).astype(bf16)
            total[...] = total[...] * jnp.exp2(old_top - new_top) + dot(values[key_at], weights, 1, 0)
            top[...] = new_top

        two_ahead(count, todo, at, fill, work)
        final = total[...]
        weight_sum = final[HEAD : HEAD + 1, :]
        mixed = final[:HEAD, :] * (1.0 / weight_sum)
        out_ref[i] = mixed.astype(bf16)
        full_ref[i] = mixed
        lse_ref[i] = three_parts(top[...] + jnp.log2(weight_sum))
        return carry

    lax.fori_loop(0, out_ref.shape[0], attend, 0)


def fwd_call(todo, seg, need, keys, values, queries):
    count, (pieces, _, piece) = todo.shape[0], queries.shape
    return call(
        fwd_kernel, "attend",
        (shape_of(count, HEAD, piece), shape_of(count, HEAD, piece, dtype=f32), shape_of(count, 16, piece)),
        (todo, seg, need, keys, values, queries),
        scratch=[pltpu.VMEM((piece, piece), f32)] * 2
        + [pltpu.VMEM((1, piece), f32), pltpu.VMEM((HEAD + 16, piece), f32), pltpu.SMEM((pieces,), jnp.int32)],
        scalars=3, mib=22,
    )


def bwd_kernel(todo_ref, place_ref, seg_ref, need_ref, cos_ref, sin_ref, keys, key_lanes, values, queries, grads, *rest, stage, todo_count, ready):
    if stage:
        kept, sum_in, rest = rest[0], rest[1], rest[2:]
    outs, rest = rest[: (2, 3, 1)[stage]], rest[(2, 3, 1)[stage] :]
    score_a, grad_a, score_b, grad_b, key_sum, value_sum, todo = rest[:7]
    sums = rest[7] if stage == 2 else outs[-1]
    pieces = queries.shape[0]
    scores, prob_grads = (score_a, score_b), (grad_a, grad_b)
    sums[...] = sum_in[...] if stage else jnp.zeros(sums.shape, f32)
    if stage == 1:
        outs[0][:2] = kept[...]
    if stage == 2:
        outs[0][2:, : 2 * HEAD, :] = kept[...]
    ready()

    def attend(i, carry):
        at = todo_ref[i]
        seg = seg_ref[at]
        count = collect(at + 1, pieces, lambda q: (need_ref[q] & seg) != 0, todo)
        key, value, key_lane = keys[at], values[at], key_lanes[at]
        score_a[...] = causal(dot(key, queries[at], 1, 0))
        grad_a[...] = dot(value, grads[at], 1, 0)
        key_sum[...] = jnp.zeros(key_sum.shape, f32)
        value_sum[...] = jnp.zeros(value_sum.shape, f32)

        def fill(slot, query_at):
            scores[slot][...] = dot(key, queries[query_at], 1, 0)
            prob_grads[slot][...] = dot(value, grads[query_at], 1, 0)

        def work(slot, query_at):
            probs = jnp.exp2(scores[slot][...])
            score_grad = (probs * prob_grads[slot][...]).astype(bf16)
            value_sum[...] += dot(grads[query_at, :HEAD, :], probs.astype(bf16), 1, 1)
            key_sum[...] += dot(queries[query_at, :HEAD, :], score_grad, 1, 1)
            sums[query_at] += dot(key_lane, score_grad, 1, 0)

        two_ahead(count, todo, at, fill, work)
        key_grad = unrotate(key_sum[...] * (1.0 / LOG2E), cos_ref[at], sin_ref[at]).astype(bf16)
        value_grad = (0.5 * value_sum[...]).astype(bf16)

        def write(ref, place):
            ref[place, :HEAD, :] = key_grad
            ref[place, HEAD : 2 * HEAD, :] = value_grad

        if stage == 1:
            pl.when(i < 2)(lambda: write(outs[0], 2 + i))
            pl.when(i >= 2)(lambda: write(outs[1], i - 2))
        else:
            write(outs[0], i)
        return carry

    lax.fori_loop(0, todo_count, attend, 0)
    if stage == 2:
        for p in range(pieces):
            grad = unrotate(sums[p] * SCORE_SCALE, cos_ref[p], sin_ref[p]).astype(bf16)
            start = pl.multiple_of((2 + ((p % 2) ^ place_ref[0])) * HEAD, HEAD)
            outs[0][p // 2, pl.ds(start, HEAD), :] = grad


def bwd_call(stage, todo, place, seg, need, cosine, sine, keys, key_lanes, values, queries, grads, kept, query_sum):
    count, (pieces, _, piece) = todo.shape[0], queries.shape
    places = pieces // 2
    sums = shape_of(pieces, HEAD, piece, dtype=f32)
    outs = (
        (shape_of(2, 2 * HEAD, piece), sums),
        (shape_of(places, 2 * HEAD, piece), shape_of(2, 2 * HEAD, piece), sums),
        (shape_of(places, 4 * HEAD, piece),),
    )[stage]
    operands = (cosine, sine, keys, key_lanes, values, queries, grads) + ((kept, query_sum) if stage else ())
    got = call(
        functools.partial(bwd_kernel, stage=stage, todo_count=count), "attend_back", outs,
        (todo, place, seg, need, *operands),
        scratch=[pltpu.VMEM((piece, piece), f32)] * 4
        + [pltpu.VMEM((HEAD, piece), f32)] * 2
        + [pltpu.SMEM((pieces,), jnp.int32)]
        + ([pltpu.VMEM(sums.shape, f32)] if stage == 2 else []),
        scalars=4, mib=36, late=(0, 1),
    )
    return got[0] if stage == 2 else got


def after(value, *earlier):
    return lax.optimization_barrier((value,) + earlier)[0]


def on_device(
    tokens, first_values, cotangent, parents, seg_lengths,
    w_query, w_key, w_value, w_out, w_gate, w_up, w_down, gain_attn, gain_ffn,
):
    assert tokens.shape[1] == 1
    fsdp_count, ctx_count, tp_count = (lax.axis_size(a) for a in ("fsdp", "ctx", "tp"))
    assert tp_count == 4 and ctx_count == 4
    fsdp_at, ctx_at, tp_at = (lax.axis_index(a) for a in ("fsdp", "ctx", "tp"))
    core_at, x_at = tp_at % 2, tp_at // 2
    own_rows, width = tokens.shape[0], tokens.shape[2]
    chip_rows = 2 * own_rows
    heads = w_query.shape[1] // HEAD
    head_width = heads * HEAD
    assert heads == ctx_count
    tree_len = own_rows * tp_count * ctx_count
    weight_rows, hidden = w_query.shape[0], w_gate.shape[1]
    two = fsdp_count == 2

    def over_core(value):
        return lax.ppermute(value, "tp", [(i, i ^ 1) for i in range(tp_count)])

    def over_x(value):
        return lax.ppermute(value, "tp", [(i, i ^ 2) for i in range(tp_count)])

    def over_fsdp(value):
        return lax.ppermute(value, "fsdp", [(0, 1), (1, 0)])

    def over_ctx(value, flip):
        return lax.ppermute(value, "ctx", [(i, i ^ flip) for i in range(ctx_count)])

    def exchange(by_place):
        return lax.all_to_all(by_place, "ctx", 0, 0, tiled=True)

    def relative(rows):
        if not two:
            return rows
        swapped = jnp.concatenate([rows[..., weight_rows:], rows[..., :weight_rows]], axis=-1)
        return jnp.where(fsdp_at == 0, rows, swapped)

    def by_x(near, far):
        return jnp.where(x_at == 0, jnp.concatenate([near, far], axis=0), jnp.concatenate([far, near], axis=0))

    def fsdp_sum(parts, axis=0):
        if not two:
            return lax.psum_scatter(parts[0], "fsdp", scatter_dimension=axis, tiled=True)
        return parts[0], over_fsdp(parts[1])

    def inward(low):
        return low, lax.ppermute(low, "ctx", [(0, 1), (3, 2)])

    def across(low):
        return low, lax.ppermute(low, "ctx", [(1, 2), (2, 1)])

    def outward(low):
        return low, lax.ppermute(low, "ctx", [(1, 0), (2, 3)])

    def join(pair):
        return (pair[0].astype(f32) + pair[1].astype(f32)).astype(bf16)

    def finish(pair):
        return jnp.where((ctx_at == 0) | (ctx_at == 3), pair[1], pair[0]).astype(f32)

    def hold(pair, *earlier):
        return (pair[0], after(pair[1], *earlier)) if isinstance(pair, tuple) else after(pair, *earlier)

    def step(*pairs):
        if not two:
            return [join(pair) if isinstance(pair, tuple) else pair for pair in pairs]
        return join_call(*pairs)

    own_tokens = tokens[:, 0, :]
    token_x = over_x(own_tokens)
    token_core = over_core(own_tokens)
    gains = jnp.stack([gain_attn, gain_ffn])
    if two:
        gains = jnp.concatenate([gains, over_fsdp(gains)], axis=1)
    else:
        gains = lax.all_gather(gains, "fsdp", axis=1, tiled=True)
    attention_gain = gains[0].reshape(1, width).astype(f32)
    ffn_gain = gains[1].reshape(1, width).astype(f32)
    three = (w_query, w_key, w_value)
    if two:
        own_three = stack_call(*three)
        qkv_weight = [own_three, over_fsdp(own_three)]
    else:
        qkv_weight = [stack_call(*(lax.all_gather(w, "fsdp", axis=0, tiled=True) for w in three))]
    count = len(qkv_weight)

    place = jnp.stack([x_at, core_at, ctx_at, fsdp_at]).astype(jnp.int32)
    position, query_extra, key_extra, seg_bits, need_bits = layout_call(parents, seg_lengths, tree_len, chip_rows)
    frequency = jnp.exp(-math.log(10000.0) * jnp.arange(HALF, dtype=f32) / HALF)
    angles = frequency[None, :, None] * position
    cosine, sine = jnp.cos(angles), jnp.sin(angles)

    def normalize(rows_f32):
        return lax.rsqrt(jnp.mean(rows_f32 * rows_f32, axis=-1, keepdims=True) + epsilon)

    first_flat = first_values[:, 0, :]

    def spread(pieces):
        return [over_ctx(piece, flip) if flip else piece for flip, piece in enumerate(pieces)]

    others = (w_gate, w_up, w_down, w_out)
    if two:
        feed_own = stack_call(*(after(w.T, own_three) for w in others))
    near_normed = norm_call(after(place, feed_own) if two else place, own_tokens, token_core, attention_gain, two)
    far_normed = norm_call(after(place, near_normed), token_x, over_core(token_x), attention_gain, two)
    if two:
        feed_weight = [feed_own, over_fsdp(feed_own)]
    else:
        feed_weight = [stack_call(*(lax.all_gather(w, "fsdp", axis=0, tiled=True).T for w in others))]
    by_head = project_call(place, near_normed, far_normed, cosine, sine, first_flat, qkv_weight)
    own_cot = relative(after(cotangent[:, 0, :], by_head))
    arrived = after(place, own_cot)
    keys, key_lanes, value_lanes, values, queries = prep_call(arrived, query_extra, key_extra, exchange(by_head))
    cot_x = over_x(after(own_cot, keys))
    out_weight = pick_call([after(w, keys) for w in feed_weight], head_width)
    out_weight_x = over_x(out_weight)
    cot_core = over_core(after(own_cot, keys))
    cot_x_core = over_core(cot_x)

    half_places = jnp.arange(ctx_count, dtype=jnp.int32) * 2
    far_out, far_full, far_lse = fwd_call(
        after(half_places + (1 - x_at), cot_core), seg_bits, need_bits, keys, value_lanes, queries
    )
    near_out, near_full, near_lse = fwd_call(
        after(half_places + x_at, far_out, out_weight, cot_x), seg_bits, need_bits, keys, value_lanes, queries
    )
    far_mixed = after(exchange(far_out), near_out).reshape(head_width, chip_rows)
    far_mixed_got = over_x(far_mixed)
    near_mixed = exchange(after(near_out, far_mixed)).reshape(head_width, chip_rows)

    mine, other = output_call(place, near_mixed, far_mixed_got, out_weight, out_weight_x)
    own_single = relative(own_tokens).astype(f32)
    middle = own_single + mine + over_core(other).astype(f32)

    middle_scale = normalize(middle)
    ffn_own = (middle * middle_scale * ffn_gain).astype(bf16)
    ffn_x = over_x(ffn_own)
    ffn_core = over_core(ffn_own)
    ffn_x_core = over_core(ffn_x)
    near_hidden, near_gate, near_up, near_mine, near_sent = feed_call(
        ffn_own, ffn_core, own_cot, cot_core, feed_weight, hidden
    )
    far_hidden, far_gate, far_up, far_mine, far_sent = feed_call(
        after(ffn_x, near_mine), ffn_x_core, cot_x, cot_x_core, feed_weight, hidden
    )
    far_sum = (far_mine + over_core(far_sent).astype(f32)).astype(bf16)
    far_sum_got = over_x(far_sum)
    near_sum = near_mine + over_core(near_sent).astype(f32)

    all_cot = (after(own_cot, far_sum), cot_core, cot_x, cot_x_core)
    all_ffn = (after(ffn_own, far_sum), ffn_core, ffn_x, ffn_x_core)
    first_parts, second_parts = feed_grads_call(
        (near_gate, far_gate, near_up, far_up), (near_hidden, far_hidden), all_ffn, all_cot, count
    )
    first_sum = fsdp_sum(first_parts, 1)
    second_sum = fsdp_sum(second_parts, 1)
    ffn_grad = near_sum + after(far_sum_got, first_parts[0]).astype(f32)

    weighted = ffn_grad * ffn_gain
    middle_grad = (
        own_cot.astype(f32)
        + middle_scale * weighted
        - middle * (middle_scale**3 * jnp.mean(weighted * middle, axis=-1, keepdims=True))
    )
    middle_low = middle_grad.astype(bf16)
    near_heads, far_heads, chip_low = heads_call(place, middle_low, over_core(middle_low), out_weight, out_weight_x)
    far_out_grad = over_x(far_heads)
    near_grads = exchange(near_heads.reshape(heads, HEAD, chip_rows))
    far_grads = exchange(after(far_out_grad, near_grads).reshape(heads, HEAD, chip_rows))

    ffn_gain_part = jnp.sum(after(ffn_grad, near_heads) * middle * middle_scale, axis=0)
    low_x = over_x(after(middle_low, far_out_grad))
    low_x_core = over_core(low_x)
    near_result, far_result, sent = result_call(after(near_hidden, near_heads), far_hidden, feed_weight)
    sent_got = over_core(sent)
    far_result_low = (far_result + sent_got[1].astype(f32)).astype(bf16)
    far_result_got = over_x(far_result_low)

    (first_low,) = step(hold(first_sum, far_grads))
    first_in = inward(first_low)
    back_queries, grads = prep_back_call(
        after(place, far_result_low, first_low), queries, query_extra.shape[1], near_grads, far_grads, near_full, far_full, near_lse, far_lse
    )

    def back(stage, places, kept, query_sum, *earlier):
        return bwd_call(
            stage, after(jnp.stack(places).astype(jnp.int32), *earlier), place, seg_bits, need_bits, cosine, sine,
            keys, key_lanes, values, back_queries, grads, kept, query_sum,
        )

    far_at, near_at = [2 * i + 1 - x_at for i in range(4)], [2 * i + x_at for i in range(4)]
    first_kv, query_sum = back(0, far_at[:2], None, None, first_low)

    first_low, second_low = step(hold(first_in, first_kv), hold(second_sum, first_kv))
    first_across, second_in = across(first_low), inward(second_low)
    far_kv, near_kv, query_sum = back(1, far_at[2:] + near_at[2:], first_kv, query_sum, first_low)

    first_low, second_low = step(hold(first_across, far_kv), hold(second_in, far_kv))
    first_done, second_across = outward(first_low), across(second_low)
    far_kv_got = exchange(after(far_kv, first_low))
    last = back(2, near_at[:2], near_kv, query_sum, first_low)

    (second_low,) = step(hold(second_across, last))
    second_done = outward(second_low)
    last_got = exchange(after(last, second_low, first_done[1]))
    far_kv_got = after(far_kv_got, last)
    out_parts = out_grads_call(after(place, last), chip_low, low_x, low_x_core, near_mixed, far_mixed, count)
    out_sum = fsdp_sum(out_parts)
    second_all = finish(hold(second_done, out_parts[0]))
    layer_out = relative((after(middle, second_all) + near_result + sent_got[0].astype(f32) + far_result_got.astype(f32)).astype(bf16))
    first_all = finish(hold(first_done, second_low))
    (out_low,) = step(hold(out_sum, layer_out))
    last_got = after(last_got, first_all, out_low)
    out_in = inward(out_low)

    far_mine, far_other, far_gain = rows_call(place, far_normed, far_kv_got, last_got, qkv_weight, 1)
    far_rows_got = over_x((far_mine + over_core(far_other).astype(f32)).astype(bf16))
    near_mine, near_other, near_gain = rows_call(
        after(place, far_mine), near_normed, far_kv_got, last_got, qkv_weight, 0
    )
    near_rows_got = over_core(near_other)
    qkv_parts = weights_call(after(near_normed, near_mine), far_normed, far_kv_got, last_got, count)
    qkv_sum = fsdp_sum(qkv_parts)
    gain_sum = jnp.concatenate([(far_gain + near_gain) / attention_gain, ffn_gain_part[None]], axis=0)
    if two:
        gain_sum = gain_sum + over_core(gain_sum)
        gain_sum = gain_sum + over_x(gain_sum)
    qkv_low, out_low = step(hold(qkv_sum, gain_sum), hold(out_in, gain_sum))
    qkv_in, out_across = inward(qkv_low), across(out_low)
    near_value = after(last_got, qkv_low)[:, HEAD : 2 * HEAD].reshape(head_width, chip_rows)
    far_value = far_kv_got[:, HEAD:].reshape(head_width, chip_rows)
    grad_values = by_x(near_value.T, far_value.T).astype(f32)
    if two:
        gain_sum = gain_sum[:, :weight_rows] + over_fsdp(after(gain_sum, qkv_low)[:, weight_rows:])
        gain_sum = gain_sum + over_ctx(gain_sum, 1)
    qkv_low, out_low = step(hold(qkv_in, gain_sum, grad_values), hold(out_across, gain_sum))
    lows = [qkv_low]
    qkv_across, out_done = across(qkv_low), outward(out_low)
    if two:
        gain_sum = gain_sum + over_ctx(after(gain_sum, qkv_low), 2)
    else:
        gain_sum = lax.psum(gain_sum, ("fsdp", "ctx", "tp"))
        gain_sum = lax.dynamic_slice_in_dim(gain_sum, fsdp_at * weight_rows, weight_rows, 1)
    (qkv_low,) = step(hold(qkv_across, gain_sum, out_done[1]))
    grad_query, grad_key, grad_value = jnp.split(finish(outward(qkv_low)), 3)
    grad_out = finish(out_done)
    grad_gate, grad_up, grad_down = first_all[:hidden].T, first_all[hidden:].T, second_all.T

    normed_grad = after(near_mine, lows[0]) + near_rows_got.astype(f32) + far_rows_got.astype(f32)
    scale = normalize(own_single)
    weighted = normed_grad * attention_gain
    grad_tokens = (
        middle_grad + scale * weighted - own_single * (scale**3 * jnp.mean(weighted * own_single, axis=-1, keepdims=True))
    )
    return (
        layer_out[:, None, :],
        relative(grad_tokens)[:, None, :],
        grad_values[:, None, :],
        grad_query,
        grad_key,
        grad_value,
        grad_out,
        grad_gate,
        grad_up,
        grad_down,
        gain_sum[0],
        gain_sum[1],
    )

def solution(mesh):
    rows, columns = P(("ctx", "tp"), "fsdp", None), P("ctx", "fsdp", "tp")
    weight, gain = P("fsdp", "tp"), P("fsdp")
    return jax.shard_map(
        on_device,
        mesh=mesh,
        in_specs=(rows, columns, rows, P("fsdp", None), P("fsdp", None)) + (weight,) * 7 + (gain,) * 2,
        out_specs=(rows, rows, columns) + (weight,) * 7 + (gain,) * 2,
        check_vma=False,
    )
```

time: 583 us -> 545 us (0.935)
  Pallas kernels: 83.5 us -> 203 us
  matrix products: 56 us -> 0 us
  waiting for transfers between devices: 205 us -> 156 us
  blocking collectives: 37.3 us -> 0 us
  starting transfers between devices: 126 us -> 108 us
  other arithmetic: 30.9 us -> 43.8 us
  local copies, waits for them, and re-layouts: 30.7 us -> 23.6 us
    ppermute x61 -> x22, waiting for transfers between devices: 193 us -> 64 us  [the longest x4 36.4 us: outward(): return (low, lax.ppermute(low, 'ctx', [(1, 0), (2, 3)]))]
    pallas_call x3 -> x32, Pallas kernels: 83.5 us -> 203 us  [the longest x31 200 us: call(): pl.pallas_call(body, out_shape=outs, in_specs=[SMEM] * scalars + [pl.Bloc...]
    ppermute x61 -> x22, starting transfers between devices: 109 us -> 45.7 us  [the longest x8 16.7 us: over_fsdp(): return lax.ppermute(value, 'fsdp', [(0, 1), (1, 0)])]
    dot_general x30 -> x0, matrix products: 56 us -> none  [dot(): lax.dot_general(a, b, (((ca,), (cb,)), ((), ())), preferred_element_type=...]
    all_to_all x0 -> x7, waiting for transfers between devices: none -> 48.5 us  [exchange(): return lax.all_to_all(by_place, 'ctx', 0, 0, tiled=True)]
    all_to_all x0 -> x7, starting transfers between devices: none -> 41.2 us  [exchange(): return lax.all_to_all(by_place, 'ctx', 0, 0, tiled=True)]
    psum x1 -> x0, blocking collectives: 37.3 us -> none  [on_device(): lax.psum(jnp.stack([attention_gain_part, ffn_gain_part]), ('fsdp', 'ctx',...]
    ppermute x10 -> x11, waiting for transfers between devices: 12.3 us -> 39.2 us  [over_x(): return lax.ppermute(value, 'tp', [(i, i ^ 2) for i in range(tp_count)])]
  transfers between devices with their start and end apart: 86 -> 55, of which waited for: 34 -> 19; matrix products, arithmetic and copies ran while one was open for 19% -> 9% of each run, Pallas kernels for 15% -> 29%
where the time goes in v2:
time: 545 us; the launch traced here: 537 us
  Pallas kernels  203 us (37%)
  waiting for transfers between devices  156 us (29%)
  starting transfers between devices  108 us (20%)
  other arithmetic  43.8 us (8%)
  local copies, waits for them, and re-layouts  23.6 us (4%)
    pallas_call x31, Pallas kernels, call(): pl.pallas_call(body, out_shape=outs, in_specs=[SMEM] * scalars + [pl.Bloc...  200 us
    all_to_all x7, waiting for transfers between devices, exchange(): return lax.all_to_all(by_place, 'ctx', 0, 0, tiled=True)  48.5 us
    all_to_all x7, starting transfers between devices, exchange(): return lax.all_to_all(by_place, 'ctx', 0, 0, tiled=True)  41.2 us
    ppermute x11, waiting for transfers between devices, over_x(): return lax.ppermute(value, 'tp', [(i, i ^ 2) for i in range(tp_count)])  39.2 us
    ppermute x4, waiting for transfers between devices, outward(): return (low, lax.ppermute(low, 'ctx', [(1, 0), (2, 3)]))  36.4 us
    ppermute x11, starting transfers between devices, over_x(): return lax.ppermute(value, 'tp', [(i, i ^ 2) for i in range(tp_count)])  19.7 us
    ppermute x8, starting transfers between devices, over_fsdp(): return lax.ppermute(value, 'fsdp', [(0, 1), (1, 0)])  16.7 us
    unnamed x95, local copies, waits for them, and re-layouts  14.9 us
  transfers between devices with their start and end apart: 55, of which 19 were waited for; matrix products, arithmetic and copies ran while one was open for 9% of the time, Pallas kernels for 29%

profile of v2, /device:TPU:0, one launch (start us, length us, event | category | flops | bytes accessed | tf_op | source)
XLA Modules:
  0.0 536.8 jit_solution(15444976175239384838)
XLA Ops:
  12.5 6.1 %collective-permute-done.2.refs_1_ = bf16[320,1024]{1,0:T(8,128)(2,1)S(1)} collective-permute-done((bf16[320,1024]{1,0:T(8,128)(2,1)}, bf16[320,1024]{1,0:T(8,128)(2,1)S(1)}, u32[]{:S(2)}, u32[]{:S(2)}) %collective-permute-start.2) | collective-permute-done | bytes 655392 | tf_op jit(solution)/shard_map/ppermute | solution.py:695
  37.2 7.5 %project.1 = bf16[4,192,1280]{2,1,0:T(8,128)(2,1)} custom-call(s32[4]{0:T(128)} %pad_add_fusion.refs_0_.refs_1_, bf16[640,1024]{1,0:T(8,128)(2,1)} %normalise.2.refs_1_.refs_0_, bf16[640,1024]{1,0:T(8,128)(2,1)} %normalise.3.refs_2_.refs_1_, f32[8,32,640]{2,1,0:T(8,128)} %get-tuple-element.277.refs_3_.refs_4_, ...), custom_call_target="tpu_custom_call" | custom-call | bytes 65536 | tf_op jit(solution)/shard_map/project/pallas_call | solution.py:156
  53.0 43.4 %all-to-all-done.refs_3_ = bf16[4,192,1280]{2,1,0:T(8,128)(2,1)} async-done(((bf16[4,192,1280]{2,1,0:T(8,128)(2,1)}), bf16[4,192,1280]{2,1,0:T(8,128)(2,1)}, u32[]{:S(2)}, u32[]{:S(2)}) %all-to-all-start) | async-done | bytes 1966112 | tf_op jit(solution)/shard_map/all_to_all | solution.py:704
  104.4 12.3 %attend.2 = (bf16[4,64,640]{2,1,0:T(8,128)(2,1)}, f32[4,64,640]{2,1,0:T(8,128)}, bf16[4,16,640]{2,1,0:T(8,128)(2,1)}) custom-call(s32[4]{0:T(128)} %fusion.11.refs_0_, s32[8]{0:T(128)} %get-tuple-element.142.refs_1_.refs_2_, s32[8]{0:T(128)} %get-tuple-element.143.refs_2_.refs_3_, bf16[8,640,128]{2,1,0:T(8,128)(2,1)} %get-tuple-element.139.refs_3_.refs_6_, ...), custom_call_target="tpu_custom_call" | custom-call | bytes 65536 | tf_op jit(solution)/shard_map/attend/pallas_call | solution.py:156
  124.9 10.8 %attend.3 = (bf16[4,64,640]{2,1,0:T(8,128)(2,1)}, f32[4,64,640]{2,1,0:T(8,128)}, bf16[4,16,640]{2,1,0:T(8,128)(2,1)}) custom-call(s32[4]{0:T(128)} %fusion.12.refs_0_, s32[8]{0:T(128)} %get-tuple-element.142.refs_1_.refs_2_, s32[8]{0:T(128)} %get-tuple-element.143.refs_2_.refs_3_, bf16[8,640,128]{2,1,0:T(8,128)(2,1)} %get-tuple-element.139.refs_3_.refs_6_, ...), custom_call_target="tpu_custom_call" | custom-call | bytes 65536 | tf_op jit(solution)/shard_map/attend/pallas_call | solution.py:156
  144.5 7.4 %collective-permute-done.8.refs_2_ = bf16[256,640]{1,0:T(8,128)(2,1)S(1)} collective-permute-done((bf16[256,640]{1,0:T(8,128)(2,1)}, bf16[256,640]{1,0:T(8,128)(2,1)S(1)}, u32[]{:S(2)}, u32[]{:S(2)}) %collective-permute-start.8) | collective-permute-done | bytes 327712 | tf_op jit(solution)/shard_map/ppermute | solution.py:695
  164.0 14.5 %collective-permute-done.12.refs_0_.refs_8_ = bf16[320,1024]{1,0:T(8,128)(2,1)S(1)} collective-permute-done((bf16[320,1024]{1,0:T(8,128)(2,1)S(1)}, bf16[320,1024]{1,0:T(8,128)(2,1)S(1)}, u32[]{:S(2)}, u32[]{:S(2)}) %collective-permute-start.12) | collective-permute-done | bytes 655392 | tf_op jit(solution)/shard_map/ppermute | solution.py:695
  179.5 10.4 %feed.2 = (bf16[2,320,704]{2,1,0:T(8,128)(2,1)}, bf16[2,320,704]{2,1,0:T(8,128)(2,1)}, bf16[2,320,704]{2,1,0:T(8,128)(2,1)}, f32[320,1024]{1,0:T(8,128)}, bf16[320,1024]{1,0:T(8,128)(2,1)}) custom-call(bf16[320,1024]{1,0:T(8,128)(2,1)} %copy-done.8, bf16[320,1024]{1,0:T(8,128)(2,1)} %copy-done.16, bf16[320,1024]{1,0:T(8,128)(2,1)} %copy-done.4, ...), custom_call_target="tpu_custom_call" | custom-call | bytes 65536 | tf_op jit(solution)/shard_map/feed/pallas_call | solution.py:156
  189.9 10.9 %feed.3 = (bf16[2,320,704]{2,1,0:T(8,128)(2,1)}, bf16[2,320,704]{2,1,0:T(8,128)(2,1)}, bf16[2,320,704]{2,1,0:T(8,128)(2,1)}, f32[320,1024]{1,0:T(8,128)}, bf16[320,1024]{1,0:T(8,128)(2,1)}) custom-call(bf16[320,1024]{1,0:T(8,128)(2,1)} %copy-done.15, bf16[320,1024]{1,0:T(8,128)(2,1)} %collective-permute-done.13.refs_1_.refs_9_, ...), custom_call_target="tpu_custom_call" | custom-call | bytes 65536 | tf_op jit(solution)/shard_map/feed/pallas_call | solution.py:156
  206.6 12.2 %feed_grads.1 = (bf16[1408,512]{1,0:T(8,128)(2,1)}, bf16[1408,512]{1,0:T(8,128)(2,1)}, bf16[704,512]{1,0:T(8,128)(2,1)}, bf16[704,512]{1,0:T(8,128)(2,1)}) custom-call(bf16[2,320,704]{2,1,0:T(8,128)(2,1)} %get-tuple-element.155.refs_0_, bf16[2,320,704]{2,1,0:T(8,128)(2,1)} %get-tuple-element.158.refs_1_, bf16[2,320,704]{2,1,0:T(8,128)(2,1)} %get-tuple-element.159.refs_2_, ...), custom_call_target="tpu_custom_call" | custom-call | bytes 65536 | tf_op jit(solution)/shard_map/feed_grads/pallas_call | solution.py:156
  241.1 8.1 %collective-permute-done.20 = bf16[256,640]{1,0:T(8,128)(2,1)} collective-permute-done((bf16[256,640]{1,0:T(8,128)(2,1)}, bf16[256,640]{1,0:T(8,128)(2,1)}, u32[]{:S(2)}, u32[]{:S(2)}) %collective-permute-start.20) | collective-permute-done | bytes 327712 | tf_op jit(solution)/shard_map/ppermute | solution.py:695
  254.1 6.6 %result.1 = (f32[320,1024]{1,0:T(8,128)}, f32[320,1024]{1,0:T(8,128)}, bf16[2,320,1024]{2,1,0:T(8,128)(2,1)}) custom-call(bf16[2,320,704]{2,1,0:T(8,128)(2,1)} %get-tuple-element.178.refs_4_.refs_0_, bf16[2,320,704]{2,1,0:T(8,128)(2,1)} %get-tuple-element.162.refs_5_.refs_1_, bf16[2368,512]{1,0:T(8,128)(2,1)} %stack.76.refs_0_.refs_4_.refs_2_, ...), custom_call_target="tpu_custom_call" | custom-call | bytes 65536 | tf_op jit(solution)/shard_map/result/pallas_call | solution.py:156
  279.2 14.7 %attend_back.3 = (bf16[2,128,640]{2,1,0:T(8,128)(2,1)}, f32[8,64,640]{2,1,0:T(8,128)}) custom-call(s32[2]{0:T(128)} %pad_add_fusion.1.refs_0_, s32[4]{0:T(128)} %pad_add_fusion.refs_0_.refs_1_, s32[8]{0:T(128)} %get-tuple-element.142.refs_1_.refs_2_, s32[8]{0:T(128)} %get-tuple-element.143.refs_2_.refs_3_, f32[8,32,640]{2,1,0:T(8,128)} %get-tuple-element.277.refs_3_.refs_4_, ...), custom_call_target="tpu_custom_call" | custom-call | bytes 65536 | tf_op jit(solution)/shard_map/attend_back/pallas_call | solution.py:156
  305.5 6.0 %collective-permute-start.25 = (bf16[704,512]{1,0:T(8,128)(2,1)}, bf16[704,512]{1,0:T(8,128)(2,1)S(1)}, u32[]{:S(2)}, u32[]{:S(2)}) collective-permute-start(bf16[704,512]{1,0:T(8,128)(2,1)} %get-tuple-element.198.refs_2_), channel_id=1, source_target_pairs={{0,4},{12,8},{1,5},{13,9},{2,6},{14,10},{3,7},{15,11},{16,20},{28,... | collective-permute-start | bytes 2162696 | tf_op jit(solution)/shard_map/ppermute | solution.py:721
  312.1 17.9 %attend_back.4 = (bf16[4,128,640]{2,1,0:T(8,128)(2,1)}, bf16[2,128,640]{2,1,0:T(8,128)(2,1)}, f32[8,64,640]{2,1,0:T(8,128)}) custom-call(s32[4]{0:T(128)} %pad_add_fusion.2.refs_0_, s32[4]{0:T(128)} %pad_add_fusion.refs_0_.refs_1_, s32[8]{0:T(128)} %get-tuple-element.142.refs_1_.refs_2_, s32[8]{0:T(128)} %get-tuple-element.143.refs_2_.refs_3_, ...), custom_call_target="tpu_custom_call" | custom-call | bytes 65536 | tf_op jit(solution)/shard_map/attend_back/pallas_call | solution.py:156
  339.5 14.3 %all-to-all-start.5 = ((bf16[4,128,640]{2,1,0:T(8,128)(2,1)}), bf16[4,128,640]{2,1,0:T(8,128)(2,1)S(1)}, u32[]{:S(2)}, u32[]{:S(2)}) async-start(bf16[4,128,640]{2,1,0:T(8,128)(2,1)} %get-tuple-element.213), calls=%async_computation.5 | async-start | bytes 1310720 | tf_op jit(solution)/shard_map/all_to_all | solution.py:704
  354.4 17.0 %attend_back.5 = bf16[4,256,640]{2,1,0:T(8,128)(2,1)} custom-call(s32[2]{0:T(128)} %pad_add_fusion.3.refs_0_, s32[4]{0:T(128)} %pad_add_fusion.refs_0_.refs_1_, s32[8]{0:T(128)} %get-tuple-element.142.refs_1_.refs_2_, s32[8]{0:T(128)} %get-tuple-element.143.refs_2_.refs_3_, f32[8,32,640]{2,1,0:T(8,128)} %get-tuple-element.277.refs_3_.refs_4_, ...), custom_call_target="tpu_custom_call" | custom-call | bytes 65536 | tf_op jit(solution)/shard_map/attend_back/pallas_call | solution.py:156
  375.3 10.7 %collective-permute-done.31 = bf16[1408,512]{1,0:T(8,128)(2,1)} collective-permute-done((bf16[1408,512]{1,0:T(8,128)(2,1)}, bf16[1408,512]{1,0:T(8,128)(2,1)}, u32[]{:S(2)}, u32[]{:S(2)}) %collective-permute-start.31) | collective-permute-done | bytes 1441824 | tf_op jit(solution)/shard_map/ppermute | solution.py:727
  402.5 11.3 %collective-permute-done.27 = bf16[704,512]{1,0:T(8,128)(2,1)} collective-permute-done((bf16[704,512]{1,0:T(8,128)(2,1)}, bf16[704,512]{1,0:T(8,128)(2,1)}, u32[]{:S(2)}, u32[]{:S(2)}) %collective-permute-start.27) | collective-permute-done | bytes 720928 | tf_op jit(solution)/shard_map/ppermute | solution.py:727
  438.7 6.0 %weight_grads.1 = (bf16[1536,256]{1,0:T(8,128)(2,1)}, bf16[1536,256]{1,0:T(8,128)(2,1)}) custom-call(bf16[640,1024]{1,0:T(8,128)(2,1)} %normalise.2.refs_1_.refs_0_, bf16[640,1024]{1,0:T(8,128)(2,1)} %normalise.3.refs_2_.refs_1_, bf16[4,128,640]{2,1,0:T(8,128)(2,1)} %copy-done.6, bf16[4,256,640]{2,1,0:T(8,128)(2,1)} %copy-done.1), custom_call_target="tpu_custom_call" | custom-call | bytes 65536 | tf_op jit(solution)/shard_map/weight_grads/pallas_call | solution.py:156
  456.1 9.3 %collective-permute-done.33.refs_1_ = bf16[1536,256]{1,0:T(8,128)(2,1)} collective-permute-done((bf16[1536,256]{1,0:T(8,128)(2,1)}, bf16[1536,256]{1,0:T(8,128)(2,1)}, u32[]{:S(2)}, u32[]{:S(2)}) %collective-permute-start.33) | collective-permute-done | bytes 786464 | tf_op jit(solution)/shard_map/ppermute | solution.py:698
  480.2 7.1 %fusion.4 = f32[1280,1,256]{2,1,0:T(1,128)} fusion(pred[]{:T(512)S(6)} %eq.13, bf16[640,1,256]{2,1,0:T(2,128)(2,1)S(1)} %concatenate.49, bf16[640,1,256]{2,1,0:T(2,128)(2,1)S(1)} %concatenate.48), kind=kLoop, calls=%fused_computation.12 | loop fusion | flops 1310720 | bytes 1966081 | tf_op jit(solution)/shard_map/convert_element_type | solution.py:906
  501.8 10.9 %collective-permute-done.45 = f32[2,512]{1,0:T(2,128)S(1)} collective-permute-done((f32[2,512]{1,0:T(2,128)S(1)}, f32[2,512]{1,0:T(2,128)S(1)}, u32[]{:S(2)}, u32[]{:S(2)}) %collective-permute-start.45) | collective-permute-done | bytes 4128 | tf_op jit(solution)/shard_map/ppermute | solution.py:701
  520.7 14.4 %collective-permute-done.47 = bf16[1536,256]{1,0:T(8,128)(2,1)S(1)} collective-permute-done((bf16[1536,256]{1,0:T(8,128)(2,1)}, bf16[1536,256]{1,0:T(8,128)(2,1)S(1)}, u32[]{:S(2)}, u32[]{:S(2)}) %collective-permute-start.47) | collective-permute-done | bytes 786464 | tf_op jit(solution)/shard_map/ppermute | solution.py:727
  (271 shorter events, 245.0 us)
Async XLA Ops:
  3.6 23.7 %collective-permute-start = (bf16[320,1024]{1,0:T(8,128)(2,1)}, bf16[320,1024]{1,0:T(8,128)(2,1)S(1)}, u32[]{:S(2)}, u32[]{:S(2)}) collective-permute-start(bf16[320,1024]{1,0:T(8,128)(2,1)} %bitcast.57), channel_id=1, source_target_pairs={{0,1},{1,0},{2,3},{3,2},{4,5},{5,4},{6,7},{7,6},{8,9},{9,8},{10,11... | collective-permute-start | bytes 1966088 | tf_op jit(solution)/shard_map/ppermute | solution.py:692
  5.0 21.7 %collective-permute-start.1 = (bf16[2,512]{1,0:T(2,128)(2,1)S(1)}, bf16[2,512]{1,0:T(2,128)(2,1)S(1)}, u32[]{:S(2)}, u32[]{:S(2)}) collective-permute-start(bf16[2,512]{1,0:T(2,128)(2,1)S(1)} %pad_maximum_fusion.2), channel_id=1, source_target_pairs={{0,16},{16,0},{1,17},{17,1},{2,18},{18,2},{3,19},{19,3},{4,20},{20... | collective-permute-start | bytes 6152 | tf_op jit(solution)/shard_map/ppermute | solution.py:698
  8.7 27.7 %collective-permute-start.4 = (bf16[1536,256]{1,0:T(8,128)(2,1)}, bf16[1536,256]{1,0:T(8,128)(2,1)S(1)}, u32[]{:S(2)}, u32[]{:S(2)}) collective-permute-start(bf16[1536,256]{1,0:T(8,128)(2,1)} %stack.75.refs_6_.refs_4_), channel_id=1, source_target_pairs={{0,16},{16,0},{1,17},{17,1},{2,18},{18,2},{3,19},{19,3},{4,20},{20... | collective-permute-start | bytes 2359304 | tf_op jit(solution)/shard_map/ppermute | solution.py:698
  44.8 51.6 %all-to-all-start = ((bf16[4,192,1280]{2,1,0:T(8,128)(2,1)}), bf16[4,192,1280]{2,1,0:T(8,128)(2,1)}, u32[]{:S(2)}, u32[]{:S(2)}) async-start(bf16[4,192,1280]{2,1,0:T(8,128)(2,1)} %project.1), calls=%async_computation | async-start | bytes 3932160 | tf_op jit(solution)/shard_map/all_to_all | solution.py:704
  50.2 70.8 %collective-permute-start.6 = (bf16[2368,512]{1,0:T(8,128)(2,1)S(1)}, bf16[2368,512]{1,0:T(8,128)(2,1)}, u32[]{:S(2)}, u32[]{:S(2)}) collective-permute-start(bf16[2368,512]{1,0:T(8,128)(2,1)S(1)} %copy-done), channel_id=1, source_target_pairs={{0,16},{16,0},{1,17},{17,1},{2,18},{18,2},{3,19},{19,3},{4,20},{20... | collective-permute-start | bytes 7274504 | tf_op jit(solution)/shard_map/ppermute | solution.py:698
  102.2 22.8 %collective-permute-start.7 = (bf16[320,1024]{1,0:T(8,128)(2,1)S(1)}, bf16[320,1024]{1,0:T(8,128)(2,1)}, u32[]{:S(2)}, u32[]{:S(2)}) collective-permute-start(bf16[320,1024]{1,0:T(8,128)(2,1)S(1)} %maximum_select_fusion.2.refs_2_.refs_10_), channel_id=1, source_target_pairs={{0,2},{1,3},{2,0},{3,1},{4,6},{5,7},{6,4},{7,5},{8,10},{9,11},{10,... | collective-permute-start | bytes 1966088 | tf_op jit(solution)/shard_map/ppermute | solution.py:695
  163.5 26.4 %collective-permute-start.14 = (bf16[320,1024]{1,0:T(8,128)(2,1)}, bf16[320,1024]{1,0:T(8,128)(2,1)}, u32[]{:S(2)}, u32[]{:S(2)}) collective-permute-start(bf16[320,1024]{1,0:T(8,128)(2,1)} %collective-permute-done.7.refs_2_.refs_12_), channel_id=1, source_target_pairs={{0,1},{1,0},{2,3},{3,2},{4,5},{5,4},{6,7},{7,6},{8,9},{9,8},{10,11... | collective-permute-start | bytes 1966088 | tf_op jit(solution)/shard_map/ppermute | solution.py:692
  224.7 37.6 %collective-permute-start.16 = (bf16[1408,512]{1,0:T(8,128)(2,1)}, bf16[1408,512]{1,0:T(8,128)(2,1)}, u32[]{:S(2)}, u32[]{:S(2)}) collective-permute-start(bf16[1408,512]{1,0:T(8,128)(2,1)} %get-tuple-element.168), channel_id=1, source_target_pairs={{0,16},{16,0},{1,17},{17,1},{2,18},{18,2},{3,19},{19,3},{4,20},{20... | collective-permute-start | bytes 4325384 | tf_op jit(solution)/shard_map/ppermute | solution.py:698
  266.5 33.3 %collective-permute-start.21 = (bf16[1408,512]{1,0:T(8,128)(2,1)}, bf16[1408,512]{1,0:T(8,128)(2,1)}, u32[]{:S(2)}, u32[]{:S(2)}) collective-permute-start(bf16[1408,512]{1,0:T(8,128)(2,1)} %join.8.refs_0_), channel_id=1, source_target_pairs={{0,4},{12,8},{1,5},{13,9},{2,6},{14,10},{3,7},{15,11},{16,20},{28,... | collective-permute-start | bytes 4325384 | tf_op jit(solution)/shard_map/ppermute | solution.py:721
  269.5 24.4 %collective-permute-start.23 = (bf16[704,512]{1,0:T(8,128)(2,1)}, bf16[704,512]{1,0:T(8,128)(2,1)}, u32[]{:S(2)}, u32[]{:S(2)}) collective-permute-start(bf16[704,512]{1,0:T(8,128)(2,1)} %get-tuple-element.191), channel_id=1, source_target_pairs={{0,16},{16,0},{1,17},{17,1},{2,18},{18,2},{3,19},{19,3},{4,20},{20... | collective-permute-start | bytes 2162696 | tf_op jit(solution)/shard_map/ppermute | solution.py:698
  303.7 27.3 %collective-permute-start.24 = (bf16[1408,512]{1,0:T(8,128)(2,1)}, bf16[1408,512]{1,0:T(8,128)(2,1)}, u32[]{:S(2)}, u32[]{:S(2)}) collective-permute-start(bf16[1408,512]{1,0:T(8,128)(2,1)} %get-tuple-element.193.refs_0_), channel_id=1, source_target_pairs={{4,8},{8,4},{5,9},{9,5},{6,10},{10,6},{7,11},{11,7},{20,24},{24,20... | collective-permute-start | bytes 4325384 | tf_op jit(solution)/shard_map/ppermute | solution.py:724
  305.5 24.5 %collective-permute-start.25 = (bf16[704,512]{1,0:T(8,128)(2,1)}, bf16[704,512]{1,0:T(8,128)(2,1)S(1)}, u32[]{:S(2)}, u32[]{:S(2)}) collective-permute-start(bf16[704,512]{1,0:T(8,128)(2,1)} %get-tuple-element.198.refs_2_), channel_id=1, source_target_pairs={{0,4},{12,8},{1,5},{13,9},{2,6},{14,10},{3,7},{15,11},{16,20},{28,... | collective-permute-start | bytes 2162696 | tf_op jit(solution)/shard_map/ppermute | solution.py:721
  335.0 51.1 %collective-permute-start.31 = (bf16[1408,512]{1,0:T(8,128)(2,1)}, bf16[1408,512]{1,0:T(8,128)(2,1)}, u32[]{:S(2)}, u32[]{:S(2)}) collective-permute-start(bf16[1408,512]{1,0:T(8,128)(2,1)} %get-tuple-element.201), channel_id=1, source_target_pairs={{4,0},{8,12},{5,1},{9,13},{6,2},{10,14},{7,3},{11,15},{20,16},{24,... | collective-permute-start | bytes 4325384 | tf_op jit(solution)/shard_map/ppermute | solution.py:727
  336.3 35.2 %collective-permute-start.26 = (bf16[704,512]{1,0:T(8,128)(2,1)}, bf16[704,512]{1,0:T(8,128)(2,1)}, u32[]{:S(2)}, u32[]{:S(2)}) collective-permute-start(bf16[704,512]{1,0:T(8,128)(2,1)} %get-tuple-element.200.refs_0_), channel_id=1, source_target_pairs={{4,8},{8,4},{5,9},{9,5},{6,10},{10,6},{7,11},{11,7},{20,24},{24,20... | collective-permute-start | bytes 2162696 | tf_op jit(solution)/shard_map/ppermute | solution.py:724
  337.8 37.4 %collective-permute-start.28 = (bf16[320,1024]{1,0:T(8,128)(2,1)S(1)}, bf16[320,1024]{1,0:T(8,128)(2,1)}, u32[]{:S(2)}, u32[]{:S(2)}) collective-permute-start(bf16[320,1024]{1,0:T(8,128)(2,1)S(1)} %copy-done.20), channel_id=1, source_target_pairs={{0,2},{1,3},{2,0},{3,1},{4,6},{5,7},{6,4},{7,5},{8,10},{9,11},{10,... | collective-permute-start | bytes 1966088 | tf_op jit(solution)/shard_map/ppermute | solution.py:695
  339.5 49.9 %all-to-all-start.5 = ((bf16[4,128,640]{2,1,0:T(8,128)(2,1)}), bf16[4,128,640]{2,1,0:T(8,128)(2,1)S(1)}, u32[]{:S(2)}, u32[]{:S(2)}) async-start(bf16[4,128,640]{2,1,0:T(8,128)(2,1)} %get-tuple-element.213), calls=%async_computation.5 | async-start | bytes 1310720 | tf_op jit(solution)/shard_map/all_to_all | solution.py:704
  373.9 39.9 %collective-permute-start.27 = (bf16[704,512]{1,0:T(8,128)(2,1)}, bf16[704,512]{1,0:T(8,128)(2,1)}, u32[]{:S(2)}, u32[]{:S(2)}) collective-permute-start(bf16[704,512]{1,0:T(8,128)(2,1)} %join.11), channel_id=1, source_target_pairs={{4,0},{8,12},{5,1},{9,13},{6,2},{10,14},{7,3},{11,15},{20,16},{24,... | collective-permute-start | bytes 2162696 | tf_op jit(solution)/shard_map/ppermute | solution.py:727
  375.3 41.0 %collective-permute-start.30 = (bf16[320,1024]{1,0:T(8,128)(2,1)}, bf16[320,1024]{1,0:T(8,128)(2,1)}, u32[]{:S(2)}, u32[]{:S(2)}) collective-permute-start(bf16[320,1024]{1,0:T(8,128)(2,1)} %fusion.8), channel_id=1, source_target_pairs={{0,2},{1,3},{2,0},{3,1},{4,6},{5,7},{6,4},{7,5},{8,10},{9,11},{10,... | collective-permute-start | bytes 1966088 | tf_op jit(solution)/shard_map/ppermute | solution.py:695
  390.3 34.3 %all-to-all-start.6 = ((bf16[4,256,640]{2,1,0:T(8,128)(2,1)}), bf16[4,256,640]{2,1,0:T(8,128)(2,1)S(1)}, u32[]{:S(2)}, u32[]{:S(2)}) async-start(bf16[4,256,640]{2,1,0:T(8,128)(2,1)} %attend_back.5), calls=%async_computation.6 | async-start | bytes 2621440 | tf_op jit(solution)/shard_map/all_to_all | solution.py:704
  448.8 23.9 %collective-permute-start.42 = (bf16[320,1024]{1,0:T(8,128)(2,1)}, bf16[320,1024]{1,0:T(8,128)(2,1)}, u32[]{:S(2)}, u32[]{:S(2)}) collective-permute-start(bf16[320,1024]{1,0:T(8,128)(2,1)} %get-tuple-element.239), channel_id=1, source_target_pairs={{0,1},{1,0},{2,3},{3,2},{4,5},{5,4},{6,7},{7,6},{8,9},{9,8},{10,11... | collective-permute-start | bytes 1966088 | tf_op jit(solution)/shard_map/ppermute | solution.py:692
  455.1 42.0 %collective-permute-start.41 = (bf16[320,1024]{1,0:T(8,128)(2,1)}, bf16[320,1024]{1,0:T(8,128)(2,1)}, u32[]{:S(2)}, u32[]{:S(2)}) collective-permute-start(bf16[320,1024]{1,0:T(8,128)(2,1)} %get-tuple-element.238), channel_id=1, source_target_pairs={{0,1},{1,0},{2,3},{3,2},{4,5},{5,4},{6,7},{7,6},{8,9},{9,8},{10,11... | collective-permute-start | bytes 1966088 | tf_op jit(solution)/shard_map/ppermute | solution.py:692
  475.3 21.8 %collective-permute-start.43 = (bf16[320,1024]{1,0:T(8,128)(2,1)}, bf16[320,1024]{1,0:T(8,128)(2,1)}, u32[]{:S(2)}, u32[]{:S(2)}) collective-permute-start(bf16[320,1024]{1,0:T(8,128)(2,1)} %add_convert_fusion), channel_id=1, source_target_pairs={{0,2},{1,3},{2,0},{3,1},{4,6},{5,7},{6,4},{7,5},{8,10},{9,11},{10,... | collective-permute-start | bytes 1966088 | tf_op jit(solution)/shard_map/ppermute | solution.py:695
  490.1 22.7 %collective-permute-start.44 = (bf16[1536,256]{1,0:T(8,128)(2,1)}, bf16[1536,256]{1,0:T(8,128)(2,1)}, u32[]{:S(2)}, u32[]{:S(2)}) collective-permute-start(bf16[1536,256]{1,0:T(8,128)(2,1)} %get-tuple-element.236.refs_0_), channel_id=1, source_target_pairs={{4,8},{8,4},{5,9},{9,5},{6,10},{10,6},{7,11},{11,7},{20,24},{24,20... | collective-permute-start | bytes 2359304 | tf_op jit(solution)/shard_map/ppermute | solution.py:724
  491.7 21.0 %collective-permute-start.46 = (bf16[512,256]{1,0:T(8,128)(2,1)}, bf16[512,256]{1,0:T(8,128)(2,1)S(1)}, u32[]{:S(2)}, u32[]{:S(2)}) collective-permute-start(bf16[512,256]{1,0:T(8,128)(2,1)} %get-tuple-element.242), channel_id=1, source_target_pairs={{4,0},{8,12},{5,1},{9,13},{6,2},{10,14},{7,3},{11,15},{20,16},{24,... | collective-permute-start | bytes 786440 | tf_op jit(solution)/shard_map/ppermute | solution.py:727
  (79 other events, 734.6 us)
